TPU v7x, 256 devices: a whole 4x4x8 slice. The times are simulated.
256 devices in a mesh: seq: 128 (over x_lo, y, z, core), head: 2 (over x_hi).
Axes of the slice: x: 4 (x_hi: 2, x_lo: 2; x = x_hi * 2 + x_lo), y: 4, z: 8, core: 2. Of those that a mesh axis runs over, the one named last changes fastest.
Arguments:
- query: bfloat16 [32768, 3584], P('seq', 'head'), may hold values from -6 to 6
- key: bfloat16 [32768, 512], P('seq', 'head'), may hold values from -6 to 6
- value: bfloat16 [32768, 512], P('seq', 'head'), may hold values from -6 to 6
- output: bfloat16 [32768, 3584], P('seq', 'head'), may hold values from -6 to 6
- output_gradient: bfloat16 [32768, 3584], P('seq', 'head'), may hold values from -6 to 6
- lse: float32 [28, 32768], P('head', 'seq'), may hold values from 3 to 6
- doc_lengths: int32 [32], replicated, may hold values from 1 to 2048, as said below
- w_query: bfloat16 [3584, 3584], P('seq', 'head'), may hold values from -0.09375 to 0.09375
- key_weight: bfloat16 [3584, 512], P('seq', 'head'), may hold values from -0.09375 to 0.09375
- value_weight: bfloat16 [3584, 512], P('seq', 'head'), may hold values from -0.09375 to 0.09375
Outputs:
- grad_input: bfloat16 [32768, 3584], P('seq', 'head')
Inputs may be any that keep to these rules, and one draw needn't show every extreme that they name: `doc_lengths`: the documents lie end to end and fill the 32768 tokens of the pack; the first has 1024 tokens, and one of exactly 2048 tokens begins at token 15360.
All inputs are finite; a program needn't handle non-finite values.
Results may differ from a plain program's by a relative error of at most 0.0056.
Values may be sent and summed in bfloat16 or wider, within the bound.
A program may use at most 128 MiB of HBM per device.

v0:
```python
import math

import jax
import jax.numpy as jnp
from jax import lax
from jax.sharding import PartitionSpec as P

HEAD_SIZE = 128
WINDOW = 512


def shifted(array, axis, by):
    peers = lax.axis_size(axis)
    pairs = [(i, i + by) for i in range(peers) if 0 <= i + by < peers]
    return lax.ppermute(array, axis, pairs)


def lower_bounds(positions, doc_lengths, window):
    starts = jnp.cumsum(doc_lengths, dtype=jnp.int32) - doc_lengths
    inside = starts[None, :] <= positions[:, None]
    doc_begin = jnp.max(jnp.where(inside, starts[None, :], 0), axis=1)
    return jnp.maximum(doc_begin, positions - window + 1)


def attend(
    query_rows,
    key_row_block,
    value_row_block,
    visible,
    logsumexp_rows,
    output_grad_rows,
    row_delta,
    score_scale,
):
    scores = (
        jnp.einsum("tgjd,kgd->gjtk", query_rows, key_row_block, preferred_element_type=jnp.float32)
        * score_scale
    )
    prob_full = jnp.where(visible[None, None], jnp.exp(scores - logsumexp_rows[..., None]), 0.0)
    prob_low = prob_full.astype(jnp.bfloat16)
    grad_val = jnp.einsum(
        "gjtk,tgjd->kgd", prob_low, output_grad_rows, preferred_element_type=jnp.float32
    )
    grad_prob = jnp.einsum(
        "tgjd,kgd->gjtk", output_grad_rows, value_row_block, preferred_element_type=jnp.float32
    )
    dscore = (prob_full * (grad_prob - row_delta[..., None]) * score_scale).astype(jnp.bfloat16)
    grad_qry = jnp.einsum(
        "gjtk,kgd->tgjd", dscore, key_row_block, preferred_element_type=jnp.float32
    )
    grad_key = jnp.einsum("gjtk,tgjd->kgd", dscore, query_rows, preferred_element_type=jnp.float32)
    return (grad_qry, grad_key, grad_val)


def projector(grad_rows, w_piece):
    return jnp.einsum("tc,rc->tr", grad_rows, w_piece, preferred_element_type=jnp.float32)


def shards(
    query, key, value, output, output_gradient, lse, doc_lengths, w_query, key_weight, value_weight
):
    tok_rows = query.shape[0]
    key_value_width = key.shape[1]
    kv_heads = key_value_width // HEAD_SIZE
    q_heads = query.shape[1] // HEAD_SIZE
    per_group = q_heads // kv_heads
    score_scale = 1.0 / math.sqrt(HEAD_SIZE)
    seq_index = lax.axis_index("seq")
    positions = seq_index * tok_rows + jnp.arange(tok_rows, dtype=jnp.int32)
    lower = lower_bounds(positions, doc_lengths, WINDOW)
    query_rows = query.reshape(tok_rows, kv_heads, per_group, HEAD_SIZE)
    output_rows = output.reshape(tok_rows, kv_heads, per_group, HEAD_SIZE)
    output_grad_rows = output_gradient.reshape(tok_rows, kv_heads, per_group, HEAD_SIZE)
    row_delta = jnp.einsum(
        "tgjd,tgjd->gjt", output_grad_rows, output_rows, preferred_element_type=jnp.float32
    )
    logsumexp_rows = lse.reshape(kv_heads, per_group, tok_rows)
    near_pair = shifted((key, value), "seq", 1)
    far_pair = shifted((key, value), "seq", 2)
    key_all = jnp.concatenate([far_pair[0], near_pair[0], key], 0).reshape(
        3 * tok_rows, kv_heads, HEAD_SIZE
    )
    value_all = jnp.concatenate([far_pair[1], near_pair[1], value], 0).reshape(
        3 * tok_rows, kv_heads, HEAD_SIZE
    )
    key_pos = positions[0] - 2 * tok_rows + jnp.arange(3 * tok_rows, dtype=jnp.int32)
    visible = (key_pos[None, :] >= lower[:, None]) & (key_pos[None, :] <= positions[:, None])
    grad_qry, grad_key, grad_val = attend(
        query_rows,
        key_all,
        value_all,
        visible,
        logsumexp_rows,
        output_grad_rows,
        row_delta,
        score_scale,
    )
    key_parts = grad_key.reshape(3, tok_rows, key_value_width)
    value_parts = grad_val.reshape(3, tok_rows, key_value_width)
    key_far, key_near, key_own = (key_parts[0], key_parts[1], key_parts[2])
    value_far, value_near, value_own = (value_parts[0], value_parts[1], value_parts[2])
    back_near = shifted((key_near, value_near), "seq", -1)
    back_far = shifted((key_far, value_far), "seq", -2)
    key_total = key_own + back_near[0] + back_far[0]
    value_total = value_own + back_near[1] + back_far[1]
    q_grad_low = grad_qry.reshape(tok_rows, q_heads * HEAD_SIZE).astype(jnp.bfloat16)
    k_grad_low = key_total.astype(jnp.bfloat16)
    v_grad_low = value_total.astype(jnp.bfloat16)
    partial_sum = projector(q_grad_low, lax.all_gather(w_query, "seq", axis=0, tiled=True))
    partial_sum = partial_sum + projector(
        k_grad_low, lax.all_gather(key_weight, "seq", axis=0, tiled=True)
    )
    partial_sum = partial_sum + projector(
        v_grad_low, lax.all_gather(value_weight, "seq", axis=0, tiled=True)
    )
    summed = lax.psum_scatter(partial_sum, "head", scatter_dimension=1, tiled=True)
    return summed.astype(jnp.bfloat16)


def solution(mesh):
    in_specs = (
        P("seq", "head"),
        P("seq", "head"),
        P("seq", "head"),
        P("seq", "head"),
        P("seq", "head"),
        P("head", "seq"),
        P(),
        P("seq", "head"),
        P("seq", "head"),
        P("seq", "head"),
    )
    out_specs = P("seq", "head")
    return jax.shard_map(shards, mesh=mesh, in_specs=in_specs, out_specs=out_specs, check_vma=False)
```

profile of v0, /device:TPU:1, one launch (start us, length us, event | category | flops | bytes accessed | tf_op | source)
XLA Modules:
  0.0 768.8 jit_solution(6138011124968313008)
XLA Ops:
  6.5 0.7 all-gather.9.cloned.1.call-update
  7.3 0.7 all-gather.11.cloned.1.call-update
  8.1 0.7 all-gather.7.cloned.1.call-update
  8.8 1.0 copy.61
  9.8 4.9 collective-permute-start.3
  14.7 3.5 collective-permute-start.2
  18.3 1.0 copy.54
  19.3 2.2 collective-permute-start.1
  21.5 3.5 collective-permute-start
  25.1 0.6 copy-done.1
  25.6 0.5 slice.27
  26.2 0.7 sub.31
  26.9 0.7 copy.57
  27.7 0.1 reduce.1
  27.8 1.2 sub.30
  29.0 1.5 copy.64
  30.5 1.5 copy.58
  32.0 1.5 copy.93
  34.1 0.8 select_reduce_fusion
  34.9 0.9 compare_and_fusion
  35.8 0.3 fusion.9
  36.1 1.6 fusion.21
  37.7 2.4 fusion.10
  40.2 0.1 fusion.19
  40.3 1.3 collective-permute-start.7
  41.6 2.4 collective-permute-start.6
  44.0 4.0 fusion.2
  48.0 1.9 convolution_bitcast_fusion
  49.9 0.1 fusion.20
  50.0 1.3 collective-permute-start.5
  51.3 2.1 collective-permute-start.4
  53.4 0.9 convolution_convert_fusion
  54.3 0.6 collective-permute-done.6
  55.0 7.5 collective-permute-done.5
  62.5 2.8 collective-permute-done.4
  65.3 0.1 fusion.16
  65.3 172.2 %all-gather.9.cloned.1.call-done = bf16[128,28,256]{2,1,0:T(8,128)(2,1)} async-done(((bf16[1,28,256]{2,1,0:T(8,128)(2,1)}), bf16[128,28,256]{2,1,0:T(8,128)(2,1)}) %all-gather.9.cloned.1.call-update) | async-done | bytes 1835024 | tf_op jit(solution)/shard_map/all_gather | solution.py:111
  237.5 2.5 reshape.141
  240.0 210.2 %all-gather.11.cloned.1.call-done = bf16[128,28,256]{2,1,0:T(8,128)(2,1)} async-done(((bf16[1,28,256]{2,1,0:T(8,128)(2,1)}), bf16[128,28,256]{2,1,0:T(8,128)(2,1)}) %all-gather.11.cloned.1.call-update) | async-done | bytes 1835024 | tf_op jit(solution)/shard_map/all_gather | solution.py:114
  450.1 3.8 reshape.143
  453.9 222.8 %all-gather.7.cloned.1.call-done = bf16[128,28,1792]{2,1,0:T(8,128)(2,1)} async-done(((bf16[1,28,1792]{2,1,0:T(8,128)(2,1)}), bf16[128,28,1792]{2,1,0:T(8,128)(2,1)}) %all-gather.7.cloned.1.call-update) | async-done | bytes 12845072 | tf_op jit(solution)/shard_map/all_gather | solution.py:109
  676.7 17.6 %reshape.139 = bf16[3584,1792]{1,0:T(8,128)(2,1)} reshape(bf16[128,28,1792]{2,1,0:T(8,128)(2,1)} %all-gather.7.cloned.1.call-done) | data formatting | bytes 25690112
  694.3 6.6 fusion.22
  701.0 0.7 convolution_add_fusion.1
  701.7 0.8 copy-done
  702.5 2.5 convolution_add_fusion
  705.0 54.7 %reduce-scatter.2.cloned.1.call-done = f32[256,1792]{1,0:T(8,128)} async-done(((f32[256,3584]{1,0:T(8,128)}), f32[256,1792]{1,0:T(8,128)}) %reduce-scatter.2.cloned.1.call-update) | async-done | bytes 1835024 | tf_op jit(solution)/shard_map/reduce_scatter | solution.py:116
  759.7 2.5 convert_element_type.31
  (19 shorter events, 0.3 us)
Async XLA Ops:
  6.5 231.0 %all-gather.9.cloned.1.call-start = ((), (), s32[]{:S(2)}) async-start(), calls=%async_computation.3 | async-start | bytes 2113536 | tf_op jit(solution)/shard_map/all_gather | solution.py:111
  7.3 442.9 %all-gather.11.cloned.1.call-start = ((), (), s32[]{:S(2)}) async-start(), calls=%async_computation.4 | async-start | bytes 2113536 | tf_op jit(solution)/shard_map/all_gather | solution.py:114
  8.0 668.7 %all-gather.7.cloned.1.call-start = ((), (), s32[]{:S(2)}) async-start(), calls=%async_computation.2 | async-start | bytes 14794752 | tf_op jit(solution)/shard_map/all_gather | solution.py:109
  8.7 751.0 %reduce-scatter.2.cloned.1.call-start = ((), (), s32[]{:S(2)}) async-start(), calls=%async_computation.1 | async-start | bytes 5505024 | tf_op jit(solution)/shard_map/reduce_scatter | solution.py:116
  9.8 34.2 %collective-permute-start.3 = (bf16[256,256]{0,1:T(8,128)(2,1)S(1)}, bf16[256,256]{0,1:T(8,128)(2,1)S(1)}, u32[]{:S(2)}, u32[]{:S(2)}) collective-permute-start(bf16[256,256]{0,1:T(8,128)(2,1)S(1)} %copy.61), channel_id=1, source_target_pairs={{0,2},{2,4},{4,6},{6,8},{8,10},{10,12},{12,14},{14,16},{16,18},{18... | collective-permute-start | bytes 393224 | tf_op jit(solution)/shard_map/ppermute | solution.py:15
  14.7 29.3 %collective-permute-start.2 = (bf16[256,256]{0,1:T(8,128)(2,1)S(1)}, bf16[256,256]{0,1:T(8,128)(2,1)S(1)}, u32[]{:S(2)}, u32[]{:S(2)}) collective-permute-start(bf16[256,256]{0,1:T(8,128)(2,1)S(1)} %copy.61), channel_id=1, source_target_pairs={{0,4},{2,6},{4,8},{6,10},{8,12},{10,14},{12,16},{14,18},{16,20},{1... | collective-permute-start | bytes 393224 | tf_op jit(solution)/shard_map/ppermute | solution.py:15
  19.3 16.8 %collective-permute-start.1 = (bf16[256,256]{0,1:T(8,128)(2,1)S(1)}, bf16[256,256]{0,1:T(8,128)(2,1)S(1)}, u32[]{:S(2)}, u32[]{:S(2)}) collective-permute-start(bf16[256,256]{0,1:T(8,128)(2,1)S(1)} %copy.54), channel_id=1, source_target_pairs={{0,2},{2,4},{4,6},{6,8},{8,10},{10,12},{12,14},{14,16},{16,18},{18... | collective-permute-start | bytes 393224 | tf_op jit(solution)/shard_map/ppermute | solution.py:15
  21.5 14.6 %collective-permute-start = (bf16[256,256]{0,1:T(8,128)(2,1)S(1)}, bf16[256,256]{0,1:T(8,128)(2,1)S(1)}, u32[]{:S(2)}, u32[]{:S(2)}) collective-permute-start(bf16[256,256]{0,1:T(8,128)(2,1)S(1)} %copy.54), channel_id=1, source_target_pairs={{0,4},{2,6},{4,8},{6,10},{8,12},{10,14},{12,16},{14,18},{16,20},{1... | collective-permute-start | bytes 393224 | tf_op jit(solution)/shard_map/ppermute | solution.py:15
  25.1 0.6 copy-start.1
  40.3 14.0 %collective-permute-start.7 = (f32[256,256]{0,1:T(8,128)S(1)}, f32[256,256]{0,1:T(8,128)S(1)}, u32[]{:S(2)}, u32[]{:S(2)}) collective-permute-start(f32[256,256]{0,1:T(8,128)S(1)} %bitcast.104), channel_id=1, source_target_pairs={{4,0},{6,2},{8,4},{10,6},{12,8},{14,10},{16,12},{18,14},{20,16},{2... | collective-permute-start | bytes 786440 | tf_op jit(solution)/shard_map/ppermute | solution.py:15
  41.6 13.4 %collective-permute-start.6 = (f32[256,256]{0,1:T(8,128)S(1)}, f32[256,256]{0,1:T(8,128)S(1)}, u32[]{:S(2)}, u32[]{:S(2)}) collective-permute-start(f32[256,256]{0,1:T(8,128)S(1)} %bitcast.103), channel_id=1, source_target_pairs={{2,0},{4,2},{6,4},{8,6},{10,8},{12,10},{14,12},{16,14},{18,16},{20... | collective-permute-start | bytes 786440 | tf_op jit(solution)/shard_map/ppermute | solution.py:15
  50.0 12.5 %collective-permute-start.5 = (f32[256,256]{0,1:T(8,128)S(1)}, f32[256,256]{0,1:T(8,128)S(1)}, u32[]{:S(2)}, u32[]{:S(2)}) collective-permute-start(f32[256,256]{0,1:T(8,128)S(1)} %bitcast.106), channel_id=1, source_target_pairs={{4,0},{6,2},{8,4},{10,6},{12,8},{14,10},{16,12},{18,14},{20,16},{2... | collective-permute-start | bytes 786440 | tf_op jit(solution)/shard_map/ppermute | solution.py:15
  51.3 14.0 %collective-permute-start.4 = (f32[256,256]{0,1:T(8,128)S(1)}, f32[256,256]{0,1:T(8,128)S(1)}, u32[]{:S(2)}, u32[]{:S(2)}) collective-permute-start(f32[256,256]{0,1:T(8,128)S(1)} %bitcast.105), channel_id=1, source_target_pairs={{2,0},{4,2},{6,4},{8,6},{10,8},{12,10},{14,12},{16,14},{18,16},{20... | collective-permute-start | bytes 786440 | tf_op jit(solution)/shard_map/ppermute | solution.py:15
  701.0 1.5 copy-start
Sparse Core Ops, SparseCore 0:
  9.2 228.2 all-gather.8
  239.4 210.7 all-gather.10
  452.0 224.6 all-gather.6
  705.1 54.5 reduce-scatter.1
where the time goes:
time: 770 us; the launch traced here: 769 us
  waiting for transfers between devices  673 us (87%)
  local copies, waits for them, and re-layouts  33.7 us (4%)
  starting transfers between devices  21.4 us (3%)
  matrix products  20.7 us (3%)
  between operations  14.1 us (2%)
    all_gather x1, waiting for transfers between devices, shards(): lax.all_gather(w_query, 'seq', axis=0, tiled=True)  223 us
    all_gather x1, waiting for transfers between devices, shards(): lax.all_gather(value_weight, 'seq', axis=0, tiled=True)  210 us
    all_gather x1, waiting for transfers between devices, shards(): lax.all_gather(key_weight, 'seq', axis=0, tiled=True)  172 us
    reduce_scatter x1, waiting for transfers between devices, shards(): lax.psum_scatter(partial_sum, 'head', scatter_dimension=1, tiled=True)  54.7 us
    unnamed x12, local copies, waits for them, and re-layouts  31.6 us
    ppermute x8, starting transfers between devices, shifted(): return lax.ppermute(array, axis, pairs)  21.3 us
  transfers between devices with their start and end apart: 12, of which 7 were waited for; matrix products, arithmetic and copies ran while one was open for 4% of the time, Pallas kernels for 0%

commit v1 on v0

--- a/solution.py
+++ b/solution.py
@@ -106,13 +106,10 @@
     q_grad_low = grad_qry.reshape(tok_rows, q_heads * HEAD_SIZE).astype(jnp.bfloat16)
     k_grad_low = key_total.astype(jnp.bfloat16)
     v_grad_low = value_total.astype(jnp.bfloat16)
-    partial_sum = projector(q_grad_low, lax.all_gather(w_query, "seq", axis=0, tiled=True))
-    partial_sum = partial_sum + projector(
-        k_grad_low, lax.all_gather(key_weight, "seq", axis=0, tiled=True)
-    )
-    partial_sum = partial_sum + projector(
-        v_grad_low, lax.all_gather(value_weight, "seq", axis=0, tiled=True)
-    )
+    weights = jnp.concatenate([w_query, key_weight, value_weight], 1)
+    gathered = lax.all_gather(weights, "seq", axis=0, tiled=True)
+    grads = jnp.concatenate([q_grad_low, k_grad_low, v_grad_low], 1)
+    partial_sum = projector(grads, gathered)
     summed = lax.psum_scatter(partial_sum, "head", scatter_dimension=1, tiled=True)
     return summed.astype(jnp.bfloat16)
 

time: 770 us -> 355 us (0.46)
  waiting for transfers between devices: 673 us -> 255 us
    all_gather x3 -> x1, waiting for transfers between devices: 605 us -> 179 us  [shards(): gathered = lax.all_gather(weights, 'seq', axis=0, tiled=True)]
    ppermute x8, waiting for transfers between devices: 10.9 us -> 22.2 us  [shifted(): return lax.ppermute(array, axis, pairs)]
    unnamed x12 -> x8, local copies, waits for them, and re-layouts: 31.6 us -> 30.8 us
  transfers between devices with their start and end apart: 12 -> 10, of which waited for: 7 -> 6; matrix products, arithmetic and copies ran while one was open for 4% -> 6% of each run, Pallas kernels for 0% -> 0%
where the time goes in v1:
time: 355 us; the launch traced here: 354 us
  waiting for transfers between devices  255 us (72%)
  local copies, waits for them, and re-layouts  32.9 us (9%)
  matrix products  22.8 us (6%)
  starting transfers between devices  21.4 us (6%)
  between operations  14.3 us (4%)
  other arithmetic  7.59 us (2%)
    all_gather x1, waiting for transfers between devices, shards(): gathered = lax.all_gather(weights, 'seq', axis=0, tiled=True)  179 us
    reduce_scatter x1, waiting for transfers between devices, shards(): lax.psum_scatter(partial_sum, 'head', scatter_dimension=1, tiled=True)  53.8 us
    unnamed x8, local copies, waits for them, and re-layouts  30.8 us
    ppermute x8, waiting for transfers between devices, shifted(): return lax.ppermute(array, axis, pairs)  22.2 us
    ppermute x8, starting transfers between devices, shifted(): return lax.ppermute(array, axis, pairs)  21.4 us
    dot_general x1, matrix products, projector(): jnp.einsum('tc,rc->tr', grad_rows, w_piece, preferred_element_type=jnp.fl...  12 us
  transfers between devices with their start and end apart: 10, of which 6 were waited for; matrix products, arithmetic and copies ran while one was open for 6% of the time, Pallas kernels for 0%

profile of v1, /device:TPU:1, one launch (start us, length us, event | category | flops | bytes accessed | tf_op | source)
XLA Modules:
  0.0 354.0 jit_solution(8401012636219735269)
XLA Ops:
  6.5 1.6 maximum_bitcast_fusion
  8.1 0.0 all-gather.3.cloned.1.call-update
  8.2 0.0 reduce-scatter.2.cloned.1.call-start
  8.2 1.0 copy.54
  9.2 4.9 %collective-permute-start.1 = (bf16[256,256]{0,1:T(8,128)(2,1)S(1)}, bf16[256,256]{0,1:T(8,128)(2,1)S(1)}, u32[]{:S(2)}, u32[]{:S(2)}) collective-permute-start(bf16[256,256]{0,1:T(8,128)(2,1)S(1)} %copy.54), channel_id=1, source_target_pairs={{0,2},{2,4},{4,6},{6,8},{8,10},{10,12},{12,14},{14,16},{16,18},{18... | collective-permute-start | bytes 393224 | tf_op jit(solution)/shard_map/ppermute | solution.py:15
  14.2 3.5 %collective-permute-start = (bf16[256,256]{0,1:T(8,128)(2,1)S(1)}, bf16[256,256]{0,1:T(8,128)(2,1)S(1)}, u32[]{:S(2)}, u32[]{:S(2)}) collective-permute-start(bf16[256,256]{0,1:T(8,128)(2,1)S(1)} %copy.54), channel_id=1, source_target_pairs={{0,4},{2,6},{4,8},{6,10},{8,12},{10,14},{12,16},{14,18},{16,20},{1... | collective-permute-start | bytes 393224 | tf_op jit(solution)/shard_map/ppermute | solution.py:15
  17.7 1.0 copy.61
  18.7 2.2 collective-permute-start.3
  20.9 3.5 %collective-permute-start.2 = (bf16[256,256]{0,1:T(8,128)(2,1)S(1)}, bf16[256,256]{0,1:T(8,128)(2,1)S(1)}, u32[]{:S(2)}, u32[]{:S(2)}) collective-permute-start(bf16[256,256]{0,1:T(8,128)(2,1)S(1)} %copy.61), channel_id=1, source_target_pairs={{0,4},{2,6},{4,8},{6,10},{8,12},{10,14},{12,16},{14,18},{16,20},{1... | collective-permute-start | bytes 393224 | tf_op jit(solution)/shard_map/ppermute | solution.py:15
  24.5 1.5 copy.64
  26.0 1.5 copy.58
  27.4 0.7 sub.31
  28.2 0.7 copy.57
  28.9 0.1 reduce-window.9
  29.0 0.1 reduce.1
  29.1 1.2 sub.30
  30.3 0.6 copy-done
  30.8 0.5 slice.27
  31.4 1.5 copy.93
  33.5 0.8 select_reduce_fusion
  34.3 0.9 compare_and_fusion
  35.2 0.3 fusion.9
  35.5 0.0 collective-permute-done.1
  35.5 0.0 collective-permute-done
  35.5 1.6 fusion.28
  37.2 2.4 fusion.10
  39.6 0.1 fusion.27
  39.7 1.3 collective-permute-start.7
  41.0 2.4 collective-permute-start.6
  43.4 0.0 collective-permute-done.3
  43.5 4.0 %fusion.2 = bf16[2,7,256,768]{2,3,1,0:T(8,128)(2,1)S(1)} fusion(f32[2,768,256,7]{2,1,3,0:T(8,128)S(1)} %fusion.28, f32[2,7,256]{2,1,0:T(8,128)S(1)} %fusion.9, f32[2,7,256]{2,1,0:T(8,128)S(1)} %sub.31, pred[256,768]{0,1:T(8,128)(4,1)S(1)} %compare_and_fusion, bf16[768,2,128,1]{0,2,3,1:T(8,128)(2,1)S(1)} %bitcast.96, bf16[256,2,7,128]{0,3,2,1:T(8,128)(2,1)S(1)} %bitcast.91), kind=kOutput, calls=%fused_computation.3 | convolution fusion | flops 723910656 | bytes 18051072 | tf_op jit(solution)/shard_map/tgjd,kgd->gjtk/dot_general | solution.py:44
  47.5 1.9 convolution_bitcast_fusion
  49.4 0.1 fusion.26
  49.4 1.3 collective-permute-start.5
  50.7 2.1 collective-permute-start.4
  52.9 0.9 convolution_convert_fusion
  53.8 1.4 collective-permute-done.7
  55.1 10.8 %collective-permute-done.6 = f32[256,256]{0,1:T(8,128)S(1)} collective-permute-done((f32[256,256]{0,1:T(8,128)S(1)}, f32[256,256]{0,1:T(8,128)S(1)}, u32[]{:S(2)}, u32[]{:S(2)}) %collective-permute-start.6) | collective-permute-done | bytes 262176 | tf_op jit(solution)/shard_map/ppermute | solution.py:15
  66.0 0.1 fusion.20
  66.0 0.1 collective-permute-done.5
  66.1 9.9 %collective-permute-done.4 = f32[256,256]{0,1:T(8,128)S(1)} collective-permute-done((f32[256,256]{0,1:T(8,128)S(1)}, f32[256,256]{0,1:T(8,128)S(1)}, u32[]{:S(2)}, u32[]{:S(2)}) %collective-permute-start.4) | collective-permute-done | bytes 262176 | tf_op jit(solution)/shard_map/ppermute | solution.py:15
  76.1 0.1 fusion.22
  76.1 179.0 %all-gather.3.cloned.1.call-done = bf16[128,28,2304]{2,1,0:T(8,128)(2,1)} async-done(((bf16[1,28,2304]{2,1,0:T(8,128)(2,1)}), bf16[128,28,2304]{2,1,0:T(8,128)(2,1)}) %all-gather.3.cloned.1.call-update) | async-done | bytes 16515088 | tf_op jit(solution)/shard_map/all_gather | solution.py:110
  255.1 23.8 %reshape.139 = bf16[3584,2304]{1,0:T(8,128)(2,1)} reshape(bf16[128,28,2304]{2,1,0:T(8,128)(2,1)} %all-gather.3.cloned.1.call-done) | data formatting | bytes 33030144
  278.9 12.0 %fusion.13 = f32[256,3584]{1,0:T(8,128)} fusion(bf16[3584,2304]{1,0:T(8,128)(2,1)} %reshape.139, bf16[256,256]{0,1:T(8,128)(2,1)S(1)} %fusion.20, bf16[256,256]{0,1:T(8,128)(2,1)S(1)} %fusion.22, bf16[256,1792]{0,1:T(8,128)(2,1)S(1)} %bitcast.95), kind=kOutput, calls=%fused_computation.15 | convolution fusion | flops 4231397376 | bytes 21364736 | tf_op jit(solution)/shard_map/tc,rc->tr/dot_general | solution.py:56
  290.9 0.0 reduce-scatter.2.cloned.1.call-update
  290.9 53.8 %reduce-scatter.2.cloned.1.call-done = f32[256,1792]{1,0:T(8,128)} async-done(((f32[256,3584]{1,0:T(8,128)}), f32[256,1792]{1,0:T(8,128)}) %reduce-scatter.2.cloned.1.call-update) | async-done | bytes 1835024 | tf_op jit(solution)/shard_map/reduce_scatter | solution.py:113
  344.7 2.5 convert_element_type.31
  (8 shorter events, 0.1 us)
Async XLA Ops:
  6.5 248.5 %all-gather.3.cloned.1.call-start = ((), (), s32[]{:S(2)}) async-start(), calls=%async_computation.2 | async-start | bytes 19021824 | tf_op jit(solution)/shard_map/all_gather | solution.py:110
  8.2 336.5 %reduce-scatter.2.cloned.1.call-start = ((), (), s32[]{:S(2)}) async-start(), calls=%async_computation.1 | async-start | bytes 5505024 | tf_op jit(solution)/shard_map/reduce_scatter | solution.py:113
  9.2 26.2 %collective-permute-start.1 = (bf16[256,256]{0,1:T(8,128)(2,1)S(1)}, bf16[256,256]{0,1:T(8,128)(2,1)S(1)}, u32[]{:S(2)}, u32[]{:S(2)}) collective-permute-start(bf16[256,256]{0,1:T(8,128)(2,1)S(1)} %copy.54), channel_id=1, source_target_pairs={{0,2},{2,4},{4,6},{6,8},{8,10},{10,12},{12,14},{14,16},{16,18},{18... | collective-permute-start | bytes 393224 | tf_op jit(solution)/shard_map/ppermute | solution.py:15
  14.2 21.3 %collective-permute-start = (bf16[256,256]{0,1:T(8,128)(2,1)S(1)}, bf16[256,256]{0,1:T(8,128)(2,1)S(1)}, u32[]{:S(2)}, u32[]{:S(2)}) collective-permute-start(bf16[256,256]{0,1:T(8,128)(2,1)S(1)} %copy.54), channel_id=1, source_target_pairs={{0,4},{2,6},{4,8},{6,10},{8,12},{10,14},{12,16},{14,18},{16,20},{1... | collective-permute-start | bytes 393224 | tf_op jit(solution)/shard_map/ppermute | solution.py:15
  18.7 24.7 %collective-permute-start.3 = (bf16[256,256]{0,1:T(8,128)(2,1)S(1)}, bf16[256,256]{0,1:T(8,128)(2,1)S(1)}, u32[]{:S(2)}, u32[]{:S(2)}) collective-permute-start(bf16[256,256]{0,1:T(8,128)(2,1)S(1)} %copy.61), channel_id=1, source_target_pairs={{0,2},{2,4},{4,6},{6,8},{8,10},{10,12},{12,14},{14,16},{16,18},{18... | collective-permute-start | bytes 393224 | tf_op jit(solution)/shard_map/ppermute | solution.py:15
  20.9 22.5 %collective-permute-start.2 = (bf16[256,256]{0,1:T(8,128)(2,1)S(1)}, bf16[256,256]{0,1:T(8,128)(2,1)S(1)}, u32[]{:S(2)}, u32[]{:S(2)}) collective-permute-start(bf16[256,256]{0,1:T(8,128)(2,1)S(1)} %copy.61), channel_id=1, source_target_pairs={{0,4},{2,6},{4,8},{6,10},{8,12},{10,14},{12,16},{14,18},{16,20},{1... | collective-permute-start | bytes 393224 | tf_op jit(solution)/shard_map/ppermute | solution.py:15
  30.3 0.6 copy-start
  39.7 15.5 %collective-permute-start.7 = (f32[256,256]{0,1:T(8,128)S(1)}, f32[256,256]{0,1:T(8,128)S(1)}, u32[]{:S(2)}, u32[]{:S(2)}) collective-permute-start(f32[256,256]{0,1:T(8,128)S(1)} %bitcast.98), channel_id=1, source_target_pairs={{4,0},{6,2},{8,4},{10,6},{12,8},{14,10},{16,12},{18,14},{20,16},{2... | collective-permute-start | bytes 786440 | tf_op jit(solution)/shard_map/ppermute | solution.py:15
  41.0 25.0 %collective-permute-start.6 = (f32[256,256]{0,1:T(8,128)S(1)}, f32[256,256]{0,1:T(8,128)S(1)}, u32[]{:S(2)}, u32[]{:S(2)}) collective-permute-start(f32[256,256]{0,1:T(8,128)S(1)} %bitcast.97), channel_id=1, source_target_pairs={{2,0},{4,2},{6,4},{8,6},{10,8},{12,10},{14,12},{16,14},{18,16},{20... | collective-permute-start | bytes 786440 | tf_op jit(solution)/shard_map/ppermute | solution.py:15
  49.4 16.7 %collective-permute-start.5 = (f32[256,256]{0,1:T(8,128)S(1)}, f32[256,256]{0,1:T(8,128)S(1)}, u32[]{:S(2)}, u32[]{:S(2)}) collective-permute-start(f32[256,256]{0,1:T(8,128)S(1)} %bitcast.100), channel_id=1, source_target_pairs={{4,0},{6,2},{8,4},{10,6},{12,8},{14,10},{16,12},{18,14},{20,16},{2... | collective-permute-start | bytes 786440 | tf_op jit(solution)/shard_map/ppermute | solution.py:15
  50.7 25.3 %collective-permute-start.4 = (f32[256,256]{0,1:T(8,128)S(1)}, f32[256,256]{0,1:T(8,128)S(1)}, u32[]{:S(2)}, u32[]{:S(2)}) collective-permute-start(f32[256,256]{0,1:T(8,128)S(1)} %bitcast.99), channel_id=1, source_target_pairs={{2,0},{4,2},{6,4},{8,6},{10,8},{12,10},{14,12},{16,14},{18,16},{20... | collective-permute-start | bytes 786440 | tf_op jit(solution)/shard_map/ppermute | solution.py:15
Sparse Core Ops, SparseCore 0:
  9.2 245.8 all-gather.2
  291.0 53.5 reduce-scatter.1

commit v2 on v1

v2 whole, which is shorter than its diff:
```python
import functools
import math

import jax
import jax.numpy as jnp
from jax import lax
from jax.experimental import pallas as pl
from jax.experimental.pallas import tpu as pltpu
from jax.sharding import PartitionSpec as P

HEAD = 128
WINDOW = 512
NEG = -1e30
LOG2E = math.log2(math.e)
F32 = jnp.float32
BF16 = jnp.bfloat16

NY, NZ = 4, 8
LINK = 46.5e3
HOP = 1.8
NT = (((1,), (1,)), ((), ()))


def chunk_sends(part, my, mz):
    out = []
    z_up = ("z", 1, my, (mz + 1) % NZ)
    z_dn = ("z", -1, my, (mz - 1) % NZ)
    y_up = ("y", 1, (my + 1) % NY, mz)
    y_dn = ("y", -1, (my - 1) % NY, mz)
    z_ups = mz <= 3
    z_dns = mz == 0 or mz in (6, 7)
    y_ups = my <= 1
    y_dns = my == 0
    if part == 1:
        if my == 0:
            out += [z_up] if z_ups else []
            out += [z_dn] if z_dns else []
        out += [y_up] if y_ups else []
        out += [y_dn] if y_dns else []
    else:
        if mz == 0:
            out += [y_up] if y_ups else []
            out += [y_dn] if y_dns else []
        out += [z_up] if z_ups else []
        out += [z_dn] if z_dns else []
    return out


def event_plan(size0, size1):
    size = (size0, size1)
    free = {("z", 1): 0.0, ("z", -1): 0.0, ("y", 1): 0.0, ("y", -1): 0.0}
    pending = [(0.0, 1, 0, 0), (0.0, 0, 0, 0)]
    order = []
    while pending:
        pending.sort()
        t, part, my, mz = pending.pop(0)
        order.append((t, part, my, mz))
        for axis, way, ry, rz in chunk_sends(part, my, mz):
            start = max(t, free[axis, way])
            done = start + size[part] / LINK
            free[axis, way] = done
            pending.append((done + HOP, part, ry, rz))
    return order


def kernel(
    plan,
    q_hbm, k_hbm, v_hbm, o_hbm, do_hbm, lse_hbm, dl_ref, wq_hbm, wk_hbm, wv_hbm,
    out_ref,
    qv, ov, dov, kb, vb, kt, bias, stat, lse_v, dq, gt, dk, dv, gsend, grecv,
    st, stf, wa, wb, res, psend, precv, oacc,
    in_sem, kv_send, kv_recv, st_send, st_recv, ici_recv, sib_recv,
    ici_send, sib_send, g_send, g_recv, p_send, p_recv,
):
    tok = qv.shape[0]
    heads = qv.shape[1] // HEAD
    groups = kb.shape[2] // HEAD
    per = heads // groups
    rows = st.shape[1]
    half = 2 * rows
    scale = 1.0 / math.sqrt(HEAD)
    wq_w, wk_w = wq_hbm.shape[1], wk_hbm.shape[1]

    me = lax.axis_index("seq")
    hd = lax.axis_index("head")
    n = NY * NZ * 4
    core = lax.rem(me, 2)
    zc = lax.rem(me // 2, NZ)
    yc = lax.rem(me // (2 * NZ), NY)
    xc = me // (2 * NZ * NY)
    sg = 1 - 2 * core
    slot_me = yc * NZ + zc
    piece_me = xc * 2 + core

    def at(x, y, z, c):
        return ((x * NY + y) * NZ + z) * 2 + c

    def zn(d):
        return at(xc, yc, lax.rem(zc + d * sg + NZ, NZ), core)

    def yn(d):
        return at(xc, lax.rem(yc + d * sg + NY, NY), zc, core)

    def slot_of(my, mz):
        y = lax.rem(yc - my * sg + NY, NY)
        z = lax.rem(zc - mz * sg + NZ, NZ)
        return y * NZ + z

    sib = at(xc, yc, zc, 1 - core)
    xsame = at(1 - xc, yc, zc, core)
    xother = at(1 - xc, yc, zc, 1 - core)
    nxt1, nxt2 = lax.rem(me + 1, n), lax.rem(me + 2, n)
    prv1, prv2 = lax.rem(me + n - 1, n), lax.rem(me + n - 2, n)

    barrier = pltpu.get_barrier_semaphore()
    partners = [sib, xsame, xother, zn(1), zn(-1), yn(1), yn(-1), nxt1, nxt2, prv1, prv2]
    for d in partners:
        pl.semaphore_signal(barrier, inc=1, device_id={"seq": d}, device_id_type=pl.DeviceIdType.MESH)
    pl.semaphore_signal(barrier, inc=1, device_id={"head": 1 - hd}, device_id_type=pl.DeviceIdType.MESH)

    locals_ = [
        pltpu.make_async_copy(k_hbm, kb.at[0], in_sem.at[0]),
        pltpu.make_async_copy(v_hbm, vb.at[0], in_sem.at[1]),
        pltpu.make_async_copy(do_hbm, dov, in_sem.at[2]),
        pltpu.make_async_copy(o_hbm, ov, in_sem.at[3]),
        pltpu.make_async_copy(q_hbm, qv, in_sem.at[4]),
        pltpu.make_async_copy(lse_hbm, lse_v, in_sem.at[5]),
    ]
    w_src = [(wq_hbm, 0, wq_w), (wk_hbm, wq_w, wk_w), (wv_hbm, wq_w + wk_w, wk_w)]
    w_own = [
        pltpu.make_async_copy(s, st.at[piece_me, :, pl.ds(o, w)], in_sem.at[6 + j])
        for j, (s, o, w) in enumerate(w_src)
    ]
    for c in w_own + locals_:
        c.start()

    pl.semaphore_wait(barrier, len(partners) + 1)

    def remote(src, dst, ssem, rsem, dev):
        return pltpu.make_async_remote_copy(
            src_ref=src, dst_ref=dst, send_sem=ssem, recv_sem=rsem,
            device_id=dev, device_id_type=pl.DeviceIdType.MESH,
        )

    stage = []
    for pi, dev in enumerate((xsame, xother, sib)):
        for j, (s, o, w) in enumerate(w_src):
            c = remote(s, st.at[piece_me, :, pl.ds(o, w)], st_send.at[3 * pi + j], st_recv.at[3 * pi + j], {"seq": dev})
            c.start()
            stage.append(c)
    halo = []
    for b, dev in ((1, nxt1), (2, nxt2)):
        for j, (s, d) in enumerate(((k_hbm, kb), (v_hbm, vb))):
            c = remote(s, d.at[b], kv_send.at[b - 1, j], kv_recv.at[b - 1, j], {"seq": dev})
            c.start()
            halo.append(c)

    qpos = me * tok + lax.broadcasted_iota(jnp.int32, (1, tok), 1)
    low = jnp.zeros((1, tok), jnp.int32)
    start = jnp.int32(0)
    for d in range(dl_ref.shape[0]):
        low = jnp.where(qpos >= start, start, low)
        start = start + dl_ref[d]
    low = jnp.maximum(low, qpos - (WINDOW - 1))
    for b in range(3):
        kpos = (me - b) * tok + lax.broadcasted_iota(jnp.int32, (tok, tok), 0)
        ok = (kpos >= low) & (kpos <= qpos)
        bias[b] = jnp.where(ok, 0.0, NEG).astype(F32)
    dk[...] = jnp.zeros_like(dk)
    dv[...] = jnp.zeros_like(dv)
    dq[...] = jnp.zeros_like(dq)

    for c in w_own:
        c.wait()
    for c in stage:
        c.wait_recv()
    for p in range(4):
        stf[pl.ds(p * rows, rows), :] = st[p].astype(F32)
    la, lb = wa.shape[3], wb.shape[3]
    for kh in range(2):
        base = kh * (la + lb)
        wb[kh, slot_me] = stf[:, pl.ds(base + la, lb)].astype(BF16)
        wa[kh, slot_me] = stf[:, pl.ds(base, la)].astype(BF16)

    def event(part, my, mz):
        buf = wb if part == 1 else wa
        slot = slot_of(my, mz)
        ref = buf.at[core, slot]
        if (my, mz) != (0, 0):
            remote(ref, ref, ici_send.at[part], ici_recv.at[part, my, mz], {"seq": sib}).wait_recv()
        for axis, way, ry, rz in chunk_sends(part, my, mz):
            dev = zn(way) if axis == "z" else yn(way)
            remote(ref, ref, ici_send.at[part], ici_recv.at[part, ry, rz], {"seq": dev}).start()
        if (my, mz) != (0, 0):
            remote(ref, ref, sib_send.at[part], sib_recv.at[part, my, mz], {"seq": sib}).start()

    attn_at, post = plan
    for ev in attn_at[-1]:
        event(*ev)

    for c in locals_:
        c.wait()

    def delta_step(h, _):
        cols = pl.ds(pl.multiple_of(h * HEAD, HEAD), HEAD)
        prod = dov[:, cols].astype(F32) * ov[:, cols].astype(F32)
        hi = prod.astype(BF16)
        lo = (prod - hi.astype(F32)).astype(BF16)
        one = jnp.ones((8, HEAD), BF16)
        tot = lax.dot_general(one, hi, NT, preferred_element_type=F32) + lax.dot_general(one, lo, NT, preferred_element_type=F32)
        stat[h] = tot
        return 0

    lax.fori_loop(0, heads, delta_step, 0)
    lse_v[...] = lse_v[...] * LOG2E

    def grads_out(b, dev):
        for g in range(groups):
            gsend[b - 1, :, pl.ds(g * HEAD, HEAD)] = dk[b, g].astype(BF16)
            gsend[b - 1, :, pl.ds((groups + g) * HEAD, HEAD)] = dv[b, g].astype(BF16)
        return remote(gsend.at[b - 1], grecv.at[b - 1], g_send.at[b - 1], g_recv.at[b - 1], {"seq": dev})

    steps = 3 * heads

    def attn_step(it, _):
        b = it // heads
        h = lax.rem(it, heads)
        g = h // per
        for s in range(steps):
            if attn_at.get(s) or s % heads == 0:
                @pl.when(it == s)
                def _(s=s):
                    for ev in attn_at.get(s, ()):
                        event(*ev)
                    if s % heads == 0:
                        bb = s // heads
                        if bb:
                            halo[2 * (bb - 1)].wait_recv()
                            halo[2 * (bb - 1) + 1].wait_recv()
                        for gg in range(groups):
                            kt[gg] = kb[bb, :, pl.ds(gg * HEAD, HEAD)].astype(F32).T.astype(BF16)
                        if bb == 2:
                            grads_out(1, prv1).start()
        cols = pl.ds(pl.multiple_of(h * HEAD, HEAD), HEAD)
        gcols = pl.ds(pl.multiple_of(g * HEAD, HEAD), HEAD)
        qh = qv[:, cols]
        doh = dov[:, cols]
        sc = lax.dot_general(kb[b, :, gcols], qh, NT, preferred_element_type=F32)
        p = jnp.exp2((sc * (scale * LOG2E) - lse_v[pl.ds(h, 1), :]) + bias[b])
        dv[b, g] += jnp.dot(p.astype(BF16), doh, preferred_element_type=F32)
        dp = lax.dot_general(vb[b, :, gcols], doh, NT, preferred_element_type=F32)
        ds = (p * (dp - stat[h, pl.ds(0, 1), :]) * scale).astype(BF16)
        dk[b, g] += jnp.dot(ds, qh, preferred_element_type=F32)
        dq[h] += jnp.dot(kt[g], ds, preferred_element_type=F32)
        return 0

    lax.fori_loop(0, steps, attn_step, 0)
    grads_out(2, prv2).start()

    def to_gt(h, _):
        gt[pl.ds(pl.multiple_of(h * HEAD, HEAD), HEAD), :] = dq[h].astype(BF16)
        return 0

    lax.fori_loop(0, heads, to_gt, 0)

    early, by_group = post
    for ev in early:
        event(*ev)
    for b in (1, 2):
        remote(gsend.at[b - 1], grecv.at[b - 1], g_send.at[b - 1], g_recv.at[b - 1], {"seq": sib}).wait_recv()
    for j, acc in enumerate((dk, dv)):
        for g in range(groups):
            c0 = pl.ds((j * groups + g) * HEAD, HEAD)
            tot = acc[0, g] + grecv[0, :, c0].astype(F32) + grecv[1, :, c0].astype(F32)
            gt[pl.ds((heads + j * groups + g) * HEAD, HEAD), :] = tot.T.astype(BF16)

    def group_mz(j):
        return lax.rem(jnp.where(lax.rem(j, 2) == 1, (j + 1) // 2, NZ - j // 2), NZ)

    def sib_wait(part, my, mz):
        buf = wb if part == 1 else wa
        ref = buf.at[core, slot_me]
        remote(ref, ref, sib_send.at[part], sib_recv.at[part, my, mz], {"seq": sib}).wait_recv()

    def project(j, _):
        for jj in range(NZ):
            @pl.when(j == jj)
            def _(jj=jj):
                mzs = (jj + 1) // 2 if jj % 2 else (NZ - jj // 2) % NZ
                for ev in by_group[jj]:
                    event(*ev)
                for part in range(2):
                    for my in range(NY):
                        if (my, mzs) != (0, 0):
                            sib_wait(part, (NY - my) % NY, (NZ - mzs) % NZ)
        mz = group_mz(j)
        parts = []
        for my in range(NY):
            s = slot_of(my, mz)
            parts.append(jnp.concatenate([wa[0, s], wb[0, s], wa[1, s], wb[1, s]], axis=1))
        lhs = jnp.concatenate(parts, axis=0)
        res[...] = jnp.dot(lhs, gt[...], preferred_element_type=F32)
        for my in range(NY):
            s = slot_of(my, mz)
            own = pl.multiple_of(my * 2 * half + half * hd, 8)
            oth = pl.multiple_of(my * 2 * half + half * (1 - hd), 8)
            oacc[pl.ds(pl.multiple_of(s * half, 8), half), :] = res[pl.ds(own, half), :]
            psend[j, my] = res[pl.ds(oth, half), :].astype(BF16)
        remote(psend.at[j], precv.at[j], p_send.at[j], p_recv.at[j], {"head": 1 - hd}).start()
        return 0

    lax.fori_loop(0, NZ, project, 0)

    def finish(j, _):
        remote(psend.at[j], precv.at[j], p_send.at[j], p_recv.at[j], {"head": 1 - hd}).wait_recv()
        mz = group_mz(j)
        for my in range(NY):
            r = pl.ds(pl.multiple_of(slot_of(my, mz) * half, 8), half)
            oacc[r, :] = oacc[r, :] + precv[j, my].astype(F32)
        return 0

    lax.fori_loop(0, NZ, finish, 0)

    def flip(k, _):
        c = pl.ds(pl.multiple_of(k * HEAD, HEAD), HEAD)
        out_ref[:, c] = oacc[c, :].T.astype(BF16)
        return 0

    lax.fori_loop(0, oacc.shape[0] // HEAD, flip, 0)

    for c in stage + halo:
        c.wait_send()
    for part, buf in ((0, wa), (1, wb)):
        many = buf.at[0, pl.ds(0, NY * NZ - 1)]
        for sem in (ici_send, sib_send):
            remote(many, many, sem.at[part], ici_recv.at[part, 0, 0], {"seq": sib}).wait_send()
    for b in (1, 2):
        remote(gsend.at[b - 1], grecv.at[b - 1], g_send.at[b - 1], g_recv.at[b - 1], {"seq": sib}).wait_send()
    for j in range(NZ):
        remote(psend.at[j], precv.at[j], p_send.at[j], p_recv.at[j], {"head": 1 - hd}).wait_send()


def make_plan(size0, size1, steps, attn_start, attn_us, gt_ready):
    order = event_plan(size0, size1)
    attn_at = {-1: []}
    early = []
    late = [[] for _ in range(NZ)]
    rank = {0: 0, 1: 1, 7: 2, 2: 3, 6: 4, 3: 5, 5: 6, 4: 7}
    left = []
    for t, part, my, mz in order:
        s = math.ceil((t - attn_start) / attn_us)
        if s <= 0:
            attn_at.setdefault(-1 if (my, mz) == (0, 0) else 0, []).append((part, my, mz))
        elif s < steps:
            attn_at.setdefault(s, []).append((part, my, mz))
        elif t < gt_ready:
            early.append((part, my, mz))
        else:
            left.append((part, my, mz))
    pos = 0
    for j in range(NZ):
        need = -1
        for i, (part, my, mz) in enumerate(left):
            if rank[mz] <= j or rank[(NZ - mz) % NZ] <= j:
                need = i
        while pos <= need:
            late[j].append(left[pos])
            pos += 1
    assert pos == len(left)
    return attn_at, (early, late)


def shards(query, key, value, output, output_gradient, lse, doc_lengths, w_query, key_weight, value_weight):
    tok = query.shape[0]
    heads = query.shape[1] // HEAD
    groups = key.shape[1] // HEAD
    rows = w_query.shape[0]
    kdim = w_query.shape[1] + key_weight.shape[1] + value_weight.shape[1]
    la = kdim // 6
    lb = kdim // 3
    slots = NY * NZ
    plan = make_plan(4 * rows * la * 2, 4 * rows * lb * 2, 3 * heads, 3.0, 0.4, 30.0)
    any_ = pl.BlockSpec(memory_space=pl.ANY)
    vmem = pl.BlockSpec(memory_space=pltpu.VMEM)
    dma = pltpu.SemaphoreType.DMA
    return pl.pallas_call(
        functools.partial(kernel, plan),
        out_shape=jax.ShapeDtypeStruct((tok, query.shape[1]), BF16),
        in_specs=[any_] * 6 + [pl.BlockSpec(memory_space=pltpu.SMEM)] + [any_] * 3,
        out_specs=vmem,
        scratch_shapes=[
            pltpu.VMEM((tok, heads * HEAD), BF16),
            pltpu.VMEM((tok, heads * HEAD), BF16),
            pltpu.VMEM((tok, heads * HEAD), BF16),
            pltpu.VMEM((3, tok, groups * HEAD), BF16),
            pltpu.VMEM((3, tok, groups * HEAD), BF16),
            pltpu.VMEM((groups, HEAD, tok), BF16),
            pltpu.VMEM((3, tok, tok), F32),
            pltpu.VMEM((heads, 8, tok), F32),
            pltpu.VMEM((heads, tok), F32),
            pltpu.VMEM((heads, HEAD, tok), F32),
            pltpu.VMEM((kdim, tok), BF16),
            pltpu.VMEM((3, groups, tok, HEAD), F32),
            pltpu.VMEM((3, groups, tok, HEAD), F32),
            pltpu.VMEM((2, tok, 2 * groups * HEAD), BF16),
            pltpu.VMEM((2, tok, 2 * groups * HEAD), BF16),
            pltpu.VMEM((4, rows, kdim), BF16),
            pltpu.VMEM((4 * rows, kdim), F32),
            pltpu.VMEM((2, slots, 4 * rows, la), BF16),
            pltpu.VMEM((2, slots, 4 * rows, lb), BF16),
            pltpu.VMEM((NY * 4 * rows, tok), F32),
            pltpu.VMEM((NZ, NY, 2 * rows, tok), BF16),
            pltpu.VMEM((NZ, NY, 2 * rows, tok), BF16),
            pltpu.VMEM((slots * 2 * rows, tok), F32),
            dma((9,)), dma((2, 2)), dma((2, 2)), dma((9,)), dma((9,)),
            dma((2, NY, NZ)), dma((2, NY, NZ)),
            dma((2,)), dma((2,)), dma((2,)), dma((2,)), dma((NZ,)), dma((NZ,)),
        ],
        compiler_params=pltpu.CompilerParams(
            collective_id=0, has_side_effects=True, vmem_limit_bytes=60 * 1024 * 1024
        ),
    )(query, key, value, output, output_gradient, lse, doc_lengths, w_query, key_weight, value_weight)


def solution(mesh):
    both = P("seq", "head")
    in_specs = (both,) * 5 + (P("head", "seq"), P()) + (both,) * 3
    return jax.shard_map(shards, mesh=mesh, in_specs=in_specs, out_specs=both, check_vma=False)
```

time: 355 us -> 106 us (0.30)
  waiting for transfers between devices: 255 us -> 0 us
  Pallas kernels: 0 us -> 103 us
  local copies, waits for them, and re-layouts: 32.9 us -> 2.16 us
  matrix products: 22.8 us -> 0 us
  starting transfers between devices: 21.4 us -> 0 us
  between operations: 14.3 us -> 0.01 us
  other arithmetic: 7.59 us -> 0 us
    all_gather x1 -> x0, waiting for transfers between devices: 179 us -> none  [shards(): gathered = lax.all_gather(weights, 'seq', axis=0, tiled=True)]
    pallas_call x0 -> x1, Pallas kernels: none -> 103 us  [shards(): pl.pallas_call(functools.partial(kernel, plan), out_shape=jax.ShapeDtypeS...]
    reduce_scatter x1 -> x0, waiting for transfers between devices: 53.8 us -> none  [shards(): lax.psum_scatter(partial_sum, 'head', scatter_dimension=1, tiled=True)]
    unnamed x8 -> x1, local copies, waits for them, and re-layouts: 30.8 us -> 2.16 us
    dot_general x6 -> x0, matrix products: 22.8 us -> none  [the longest x1 12 us: projector(): jnp.einsum('tc,rc->tr', grad_rows, w_piece, preferred_element_type=jnp.fl...]
    ppermute x8 -> x0, waiting for transfers between devices: 22.2 us -> none  [shifted(): return lax.ppermute(array, axis, pairs)]
    ppermute x8 -> x0, starting transfers between devices: 21.4 us -> none  [shifted(): return lax.ppermute(array, axis, pairs)]
  transfers between devices with their start and end apart: 10 -> 0, of which waited for: 6 -> 0; matrix products, arithmetic and copies ran while one was open for 6% -> 0% of each run, Pallas kernels for 0% -> 0%
where the time goes in v2:
time: 106 us; the launch traced here: 105 us
  Pallas kernels  103 us (97%)
  local copies, waits for them, and re-layouts  2.16 us (2%)
    pallas_call x1, Pallas kernels, shards(): pl.pallas_call(functools.partial(kernel, plan), out_shape=jax.ShapeDtypeS...  103 us
    unnamed x1, local copies, waits for them, and re-layouts  2.16 us

profile of v2, /device:TPU:1, one launch (start us, length us, event | category | flops | bytes accessed | tf_op | source)
XLA Modules:
  0.0 105.5 jit_solution(16139729540681749506)
XLA Ops:
  0.0 103.3 %shard_map.100 = bf16[256,1792]{1,0:T(8,128)(2,1)} custom-call(bf16[256,1792]{1,0:T(8,128)(2,1)} %q_hbm.1, bf16[256,256]{1,0:T(8,128)(2,1)} %k_hbm.1, bf16[256,256]{1,0:T(8,128)(2,1)} %v_hbm.1, bf16[256,1792]{1,0:T(8,128)(2,1)} %o_hbm.1, bf16[256,1792]{1,0:T(8,128)(2,1)} %do_hbm.1, f32[14,256]{1,0:T(8,128)} %lse_hbm.1, s32[32]{0:T(128)} %dl_ref.1, ...), custom_call_target="tpu_custom_call" | custom-call | tf_op jit(solution)/shard_map/pallas_call | solution.py:386
  103.3 2.2 %copy.12 = bf16[256,1792]{1,0:T(8,128)(2,1)} copy(bf16[256,1792]{1,0:T(8,128)(2,1)} %shard_map.100) | data formatting | bytes 1835008

commit v3 on v2

v3 whole, which is shorter than its diff:
```python
import functools
import math

import jax
import jax.numpy as jnp
from jax import lax
from jax.experimental import pallas as pl
from jax.experimental.pallas import tpu as pltpu
from jax.sharding import PartitionSpec as P

HEAD = 128
WINDOW = 512
NEG = -1e30
LOG2E = math.log2(math.e)
F32 = jnp.float32
BF16 = jnp.bfloat16

NY, NZ = 4, 8
LINK = 90e3
HOP = 2.0
LOOK = 4.0
NT = (((1,), (1,)), ((), ()))


def chunk_sends(part, my, mz):
    out = []
    z_up = ("z", 1, my, (mz + 1) % NZ)
    z_dn = ("z", -1, my, (mz - 1) % NZ)
    y_up = ("y", 1, (my + 1) % NY, mz)
    y_dn = ("y", -1, (my - 1) % NY, mz)
    z_ups = mz <= 3
    z_dns = mz == 0 or mz in (6, 7)
    y_ups = my <= 1
    y_dns = my == 0
    if part == 1:
        if my == 0:
            out += [z_up] if z_ups else []
            out += [z_dn] if z_dns else []
        out += [y_up] if y_ups else []
        out += [y_dn] if y_dns else []
    else:
        if mz == 0:
            out += [y_up] if y_ups else []
            out += [y_dn] if y_dns else []
        out += [z_up] if z_ups else []
        out += [z_dn] if z_dns else []
    return out


def priority(part, my, mz):
    near_z = min(mz, NZ - mz)
    near_y = min(my, NY - my)
    return near_z, near_y, part


def event_plan(size0, size1):
    size = (size0, size1)
    free = {"z": 0.0, "y": 0.0}
    queue = {"z": [], "y": []}
    ops = []

    def arrive(t, part, my, mz):
        ops.append((t, 0, "recv", part, my, mz))
        for axis, way, ry, rz in chunk_sends(part, my, mz):
            first = (part == 1) == (axis == "z")
            queue[axis].append((t, (0 if first else 1,) + priority(part, ry, rz), (part, my, mz, axis, way, ry, rz)))

    pending = []
    arrive(0.0, 1, 0, 0)
    arrive(0.0, 0, 0, 0)
    while pending or queue["z"] or queue["y"]:
        best = None
        for axis in ("z", "y"):
            if queue[axis]:
                start = max(free[axis], min(r for r, _, _ in queue[axis]))
                if best is None or start < best[0]:
                    best = (start, axis)
        if pending and (best is None or min(pending)[0] <= best[0]):
            item = min(pending)
            pending.remove(item)
            arrive(*item)
            continue
        start, axis = best
        item = min((q for q in queue[axis] if q[0] <= start), key=lambda q: q[1])
        queue[axis].remove(item)
        ready, _, send = item
        done = start + size[send[0]] / LINK
        free[axis] = done
        pending.append((done + HOP, send[0], send[5], send[6]))
        ops.append((max(ready, start - LOOK), 1, "send") + send)
    ops.sort()
    return ops


def kernel(
    plan,
    q_hbm, k_hbm, v_hbm, o_hbm, do_hbm, lse_hbm, dl_ref, wq_hbm, wk_hbm, wv_hbm,
    out_ref,
    qv, ov, dov, kb, vb, kt, bias, stat, lse_v, dq, gt, dk, dv, nsend, nrecv, gsend, grecv,
    own, st, stf, wa, wb, res, psend, precv, oacc,
    in_sem, kv_send, kv_recv, near_send, near_recv, st_send, st_recv, ici_recv, sib_recv,
    ici_send, sib_send, n_send, n_recv, g_send, g_recv, p_send, p_recv,
):
    tok = qv.shape[0]
    heads = qv.shape[1] // HEAD
    groups = kb.shape[2] // HEAD
    per = heads // groups
    rows, hw = st.shape[1], st.shape[2]
    half = 2 * rows
    scale = 1.0 / math.sqrt(HEAD)
    wq_w, wk_w = wq_hbm.shape[1], wk_hbm.shape[1]

    me = lax.axis_index("seq")
    hd = lax.axis_index("head")
    n = NY * NZ * 4
    core = lax.rem(me, 2)
    zc = lax.rem(me // 2, NZ)
    yc = lax.rem(me // (2 * NZ), NY)
    xc = me // (2 * NZ * NY)
    sg = 1 - 2 * core
    slot_me = yc * NZ + zc
    piece_me = xc * 2 + core

    def at(x, y, z, c):
        return ((x * NY + y) * NZ + z) * 2 + c

    def zn(d):
        return at(xc, yc, lax.rem(zc + d * sg + NZ, NZ), core)

    def yn(d):
        return at(xc, lax.rem(yc + d * sg + NY, NY), zc, core)

    def slot_of(my, mz):
        y = lax.rem(yc - my * sg + NY, NY)
        z = lax.rem(zc - mz * sg + NZ, NZ)
        return y * NZ + z

    sib = at(xc, yc, zc, 1 - core)
    xsame = at(1 - xc, yc, zc, core)
    xother = at(1 - xc, yc, zc, 1 - core)
    nxt, prv = lax.rem(me + 2, n), lax.rem(me + n - 2, n)

    barrier = pltpu.get_barrier_semaphore()
    partners = [sib, xsame, xother, zn(1), zn(-1), yn(1), yn(-1), nxt, prv]
    for d in partners:
        pl.semaphore_signal(barrier, inc=1, device_id={"seq": d}, device_id_type=pl.DeviceIdType.MESH)
    pl.semaphore_signal(barrier, inc=1, device_id={"head": 1 - hd}, device_id_type=pl.DeviceIdType.MESH)

    w_own = [
        pltpu.make_async_copy(wq_hbm.at[:, pl.ds(0, hw)], own.at[0], in_sem.at[6]),
        pltpu.make_async_copy(wq_hbm.at[:, pl.ds(hw, wq_w - hw)], own.at[1, :, pl.ds(0, wq_w - hw)], in_sem.at[7]),
        pltpu.make_async_copy(wk_hbm, own.at[1, :, pl.ds(wq_w - hw, wk_w)], in_sem.at[8]),
        pltpu.make_async_copy(wv_hbm, own.at[1, :, pl.ds(wq_w - hw + wk_w, wk_w)], in_sem.at[9]),
    ]
    kv_own = [
        pltpu.make_async_copy(k_hbm, kb.at[0], in_sem.at[0]),
        pltpu.make_async_copy(v_hbm, vb.at[0], in_sem.at[1]),
    ]
    locals_ = [
        pltpu.make_async_copy(do_hbm, dov, in_sem.at[2]),
        pltpu.make_async_copy(o_hbm, ov, in_sem.at[3]),
        pltpu.make_async_copy(q_hbm, qv, in_sem.at[4]),
        pltpu.make_async_copy(lse_hbm, lse_v, in_sem.at[5]),
    ]
    for c in w_own + kv_own + locals_:
        c.start()

    qpos = me * tok + lax.broadcasted_iota(jnp.int32, (1, tok), 1)
    low = jnp.zeros((1, tok), jnp.int32)
    start = jnp.int32(0)
    for d in range(dl_ref.shape[0]):
        low = jnp.where(qpos >= start, start, low)
        start = start + dl_ref[d]
    low = jnp.maximum(low, qpos - (WINDOW - 1))
    for b in range(3):
        kpos = (me - b) * tok + lax.broadcasted_iota(jnp.int32, (tok, tok), 0)
        ok = (kpos >= low) & (kpos <= qpos)
        bias[b] = jnp.where(ok, 0.0, NEG).astype(F32)
    dk[...] = jnp.zeros_like(dk)
    dv[...] = jnp.zeros_like(dv)
    dq[...] = jnp.zeros_like(dq)

    for c in w_own + kv_own:
        c.wait()
    pl.semaphore_wait(barrier, len(partners) + 1)

    def remote(src, dst, ssem, rsem, dev):
        return pltpu.make_async_remote_copy(
            src_ref=src, dst_ref=dst, send_sem=ssem, recv_sem=rsem,
            device_id=dev, device_id_type=pl.DeviceIdType.MESH,
        )

    stage = [
        remote(own.at[kh], st.at[piece_me], st_send.at[j], st_recv.at[j], {"seq": dev})
        for j, (kh, dev) in enumerate(((core, xsame), (1 - core, xother), (1 - core, sib)))
    ]
    halo = [
        remote(src.at[0], src.at[2], kv_send.at[j], kv_recv.at[j], {"seq": nxt}) for j, src in enumerate((kb, vb))
    ]
    for c in stage + halo:
        c.start()
    mine_in = pltpu.make_async_copy(own.at[core], st.at[piece_me], in_sem.at[10])
    mine_in.start()

    def near_copy(j, src, b):
        return remote(src.at[b], src.at[1], near_send.at[j], near_recv.at[j], {"seq": sib})

    @pl.when(core == 0)
    def _():
        for j, src in enumerate((kb, vb)):
            near_copy(j, src, 0).start()

    for c in stage:
        c.wait_recv()
    mine_in.wait()
    la, lb = wa.shape[3], wb.shape[3]
    for p in range(4):
        stf[pl.ds(p * rows, rows), :] = st[p].astype(F32)
    wb[core, slot_me] = stf[:, pl.ds(la, lb)].astype(BF16)
    wa[core, slot_me] = stf[:, pl.ds(0, la)].astype(BF16)

    def event(kind, part, my, mz, *to):
        buf = wb if part == 1 else wa
        ref = buf.at[core, slot_of(my, mz)]
        if kind == "recv":
            if (my, mz) != (0, 0):
                remote(ref, ref, ici_send.at[part], ici_recv.at[part, my, mz], {"seq": sib}).wait_recv()
            remote(ref, ref, sib_send.at[part], sib_recv.at[part, my, mz], {"seq": sib}).start()
        else:
            axis, way, ry, rz = to
            dev = zn(way) if axis == "z" else yn(way)
            remote(ref, ref, ici_send.at[part], ici_recv.at[part, ry, rz], {"seq": dev}).start()

    attn_at, by_group = plan
    for ev in attn_at[-1]:
        event(*ev)

    for c in locals_:
        c.wait()

    def delta_step(h, _):
        cols = pl.ds(pl.multiple_of(h * HEAD, HEAD), HEAD)
        prod = dov[:, cols].astype(F32) * ov[:, cols].astype(F32)
        hi = prod.astype(BF16)
        lo = (prod - hi.astype(F32)).astype(BF16)
        one = jnp.ones((8, HEAD), BF16)
        tot = lax.dot_general(one, hi, NT, preferred_element_type=F32) + lax.dot_general(one, lo, NT, preferred_element_type=F32)
        stat[h] = tot
        return 0

    lax.fori_loop(0, heads, delta_step, 0)
    lse_v[...] = lse_v[...] * LOG2E

    near_grad = remote(nsend, nrecv, n_send, n_recv, {"seq": sib})
    far_grad = remote(gsend, grecv, g_send, g_recv, {"seq": prv})

    def cols_of(j, g):
        return pl.ds((j * groups + g) * HEAD, HEAD)

    def send_near():
        for j, acc in enumerate((dk, dv)):
            for g in range(groups):
                nsend[:, cols_of(j, g)] = acc[1, g]
        near_grad.start()

    def send_far():
        near_grad.wait_recv()
        keep = (core == 0).astype(F32)
        for j, acc in enumerate((dk, dv)):
            for g in range(groups):
                got = nrecv[:, cols_of(j, g)]
                gsend[:, cols_of(j, g)] = (acc[2, g] + jnp.where(core == 1, got, 0.0)).astype(BF16)
        far_grad.start()

    sub = ((0, 1), (2, 3), (4, 5, 6))
    outer = 3 * groups

    def attn_step(it, _):
        b = 2 - it // groups
        g = lax.rem(it, groups)
        for si, hs in enumerate(sub):
            for o in range(outer):
                todo = attn_at.get(o * len(sub) + si, ())
                first = si == 0
                far_now = o == 2 * groups and si == 2
                if todo or first or far_now:
                    @pl.when(it == o)
                    def _(o=o, todo=todo, first=first, far_now=far_now):
                        for ev in todo:
                            event(*ev)
                        bb = 2 - o // groups
                        if first:
                            if o == 0:
                                for c in halo:
                                    c.wait_recv()

                                @pl.when(core == 1)
                                def _():
                                    for j, src in enumerate((kb, vb)):
                                        near_copy(j, src, 2).start()
                            if o == groups:
                                for j, src in enumerate((kb, vb)):
                                    near_copy(j, src, 0).wait_recv()
                            if o == 2 * groups:
                                send_near()
                            if o % groups == 0:
                                for gg in range(groups):
                                    kt[gg] = kb[bb, :, pl.ds(gg * HEAD, HEAD)].astype(F32).T.astype(BF16)
                        if far_now:
                            send_far()
            gcols = pl.ds(pl.multiple_of(g * HEAD, HEAD), HEAD)
            kg, vg, ktg = kb[b, :, gcols], vb[b, :, gcols], kt[g]
            bs = bias[b]
            dvs, dks = [], []
            for hh in hs:
                h = g * per + hh
                cols = pl.ds(pl.multiple_of(h * HEAD, HEAD), HEAD)
                qh = qv[:, cols]
                doh = dov[:, cols]
                sc = lax.dot_general(kg, qh, NT, preferred_element_type=F32)
                dp = lax.dot_general(vg, doh, NT, preferred_element_type=F32)
                p = jnp.exp2((sc * (scale * LOG2E) - lse_v[pl.ds(h, 1), :]) + bs)
                ds = (p * (dp - stat[h, pl.ds(0, 1), :]) * scale).astype(BF16)
                dvs.append(jnp.dot(p.astype(BF16), doh, preferred_element_type=F32))
                dks.append(jnp.dot(ds, qh, preferred_element_type=F32))
                dq[h] += jnp.dot(ktg, ds, preferred_element_type=F32)
            dv[b, g] += sum(dvs[1:], dvs[0])
            dk[b, g] += sum(dks[1:], dks[0])
        return 0

    lax.fori_loop(0, outer, attn_step, 0)

    def to_gt(h, _):
        gt[pl.ds(pl.multiple_of(h * HEAD, HEAD), HEAD), :] = dq[h].astype(BF16)
        return 0

    lax.fori_loop(0, heads, to_gt, 0)

    far_grad.wait_recv()
    for j, acc in enumerate((dk, dv)):
        for g in range(groups):
            c0 = cols_of(j, g)
            tot = acc[0, g] + grecv[:, c0].astype(F32) + jnp.where(core == 0, nrecv[:, c0], 0.0)
            gt[pl.ds((heads + j * groups + g) * HEAD, HEAD), :] = tot.T.astype(BF16)

    def group_mz(j):
        return lax.rem(jnp.where(lax.rem(j, 2) == 1, (j + 1) // 2, NZ - j // 2), NZ)

    def sib_wait(part, my, mz):
        buf = wb if part == 1 else wa
        ref = buf.at[core, slot_me]
        remote(ref, ref, sib_send.at[part], sib_recv.at[part, my, mz], {"seq": sib}).wait_recv()

    def project(j, _):
        for jj in range(NZ):
            @pl.when(j == jj)
            def _(jj=jj):
                mzs = (jj + 1) // 2 if jj % 2 else (NZ - jj // 2) % NZ
                for ev in by_group[jj]:
                    event(*ev)
                for part in range(2):
                    for my in range(NY):
                        sib_wait(part, (NY - my) % NY, (NZ - mzs) % NZ)
        mz = group_mz(j)
        parts = []
        for my in range(NY):
            s = slot_of(my, mz)
            parts.append(jnp.concatenate([wa[0, s], wb[0, s], wa[1, s], wb[1, s]], axis=1))
        lhs = jnp.concatenate(parts, axis=0)
        res[...] = jnp.dot(lhs, gt[...], preferred_element_type=F32)
        out = []
        for my in range(NY):
            s = slot_of(my, mz)
            mine = pl.multiple_of(my * 2 * half + half * hd, 8)
            oth = pl.multiple_of(my * 2 * half + half * (1 - hd), 8)
            oacc[pl.ds(pl.multiple_of(s * half, 8), half), :] = res[pl.ds(mine, half), :]
            out.append(res[pl.ds(oth, half), :])
        psend[j] = jnp.concatenate(out, axis=0).astype(BF16)
        remote(psend.at[j], precv.at[j], p_send.at[j], p_recv.at[j], {"head": 1 - hd}).start()
        return 0

    lax.fori_loop(0, NZ, project, 0)

    def finish(j, _):
        remote(psend.at[j], precv.at[j], p_send.at[j], p_recv.at[j], {"head": 1 - hd}).wait_recv()
        mz = group_mz(j)
        got = precv[j].astype(F32)
        for my in range(NY):
            r = pl.ds(pl.multiple_of(slot_of(my, mz) * half, 8), half)
            oacc[r, :] = oacc[r, :] + got[my * half : (my + 1) * half]
        return 0

    lax.fori_loop(0, NZ, finish, 0)

    def flip(k, _):
        c = pl.ds(pl.multiple_of(k * HEAD, HEAD), HEAD)
        out_ref[:, c] = oacc[c, :].T.astype(BF16)
        return 0

    lax.fori_loop(0, oacc.shape[0] // HEAD, flip, 0)

    for c in stage + halo + [near_copy(0, kb, 0), near_copy(1, vb, 0), near_grad, far_grad]:
        c.wait_send()
    for part, buf in ((0, wa), (1, wb)):
        for sem, count in ((ici_send, NY * NZ - 1), (sib_send, NY * NZ)):
            many = buf.at[0, pl.ds(0, count)]
            remote(many, many, sem.at[part], ici_recv.at[part, 0, 0], {"seq": sib}).wait_send()
    for j in range(NZ):
        remote(psend.at[j], precv.at[j], p_send.at[j], p_recv.at[j], {"head": 1 - hd}).wait_send()


def make_plan(size0, size1, steps, attn_start, attn_us):
    order = [op[2:] for op in event_plan(size0, size1)]
    times = [op[0] for op in event_plan(size0, size1)]
    attn_at = {}
    left = []
    for t, op in zip(times, order):
        s = math.ceil((t - attn_start) / attn_us)
        if t <= 0.0:
            attn_at.setdefault(-1, []).append(op)
        elif s < steps:
            attn_at.setdefault(max(s, 0), []).append(op)
        else:
            left.append((t, op))
    early, late = [], [[] for _ in range(NZ)]
    rank = {0: 0, 1: 1, 7: 2, 2: 3, 6: 4, 3: 5, 5: 6, 4: 7}
    pos = 0
    for j in range(NZ):
        need = -1
        for i, (_, op) in enumerate(left):
            if op[0] == "recv" and (rank[op[3]] <= j or rank[(NZ - op[3]) % NZ] <= j):
                need = i
        if j == NZ - 1:
            need = len(left) - 1
        while pos <= need:
            late[j].append(left[pos][1])
            pos += 1
    return attn_at, late


def shards(query, key, value, output, output_gradient, lse, doc_lengths, w_query, key_weight, value_weight):
    tok = query.shape[0]
    heads = query.shape[1] // HEAD
    groups = key.shape[1] // HEAD
    rows = w_query.shape[0]
    kdim = w_query.shape[1] + key_weight.shape[1] + value_weight.shape[1]
    la = kdim // 6
    lb = kdim // 3
    slots = NY * NZ
    plan = make_plan(4 * rows * la * 2, 4 * rows * lb * 2, 9 * groups, 4.0, 0.9)
    any_ = pl.BlockSpec(memory_space=pl.ANY)
    vmem = pl.BlockSpec(memory_space=pltpu.VMEM)
    dma = pltpu.SemaphoreType.DMA
    return pl.pallas_call(
        functools.partial(kernel, plan),
        out_shape=jax.ShapeDtypeStruct((tok, query.shape[1]), BF16),
        in_specs=[any_] * 6 + [pl.BlockSpec(memory_space=pltpu.SMEM)] + [any_] * 3,
        out_specs=vmem,
        scratch_shapes=[
            pltpu.VMEM((tok, heads * HEAD), BF16),
            pltpu.VMEM((tok, heads * HEAD), BF16),
            pltpu.VMEM((tok, heads * HEAD), BF16),
            pltpu.VMEM((3, tok, groups * HEAD), BF16),
            pltpu.VMEM((3, tok, groups * HEAD), BF16),
            pltpu.VMEM((groups, HEAD, tok), BF16),
            pltpu.VMEM((3, tok, tok), F32),
            pltpu.VMEM((heads, 8, tok), F32),
            pltpu.VMEM((heads, tok), F32),
            pltpu.VMEM((heads, HEAD, tok), F32),
            pltpu.VMEM((kdim, tok), BF16),
            pltpu.VMEM((3, groups, tok, HEAD), F32),
            pltpu.VMEM((3, groups, tok, HEAD), F32),
            pltpu.VMEM((tok, 2 * groups * HEAD), F32),
            pltpu.VMEM((tok, 2 * groups * HEAD), F32),
            pltpu.VMEM((tok, 2 * groups * HEAD), BF16),
            pltpu.VMEM((tok, 2 * groups * HEAD), BF16),
            pltpu.VMEM((2, rows, kdim // 2), BF16),
            pltpu.VMEM((4, rows, kdim // 2), BF16),
            pltpu.VMEM((4 * rows, kdim // 2), F32),
            pltpu.VMEM((2, slots, 4 * rows, la), BF16),
            pltpu.VMEM((2, slots, 4 * rows, lb), BF16),
            pltpu.VMEM((NY * 4 * rows, tok), F32),
            pltpu.VMEM((NZ, NY * 2 * rows, tok), BF16),
            pltpu.VMEM((NZ, NY * 2 * rows, tok), BF16),
            pltpu.VMEM((slots * 2 * rows, tok), F32),
            dma((11,)), dma((2,)), dma((2,)), dma((2,)), dma((2,)), dma((3,)), dma((3,)),
            dma((2, NY, NZ)), dma((2, NY, NZ)),
            dma((2,)), dma((2,)), dma(()), dma(()), dma(()), dma(()), dma((NZ,)), dma((NZ,)),
        ],
        compiler_params=pltpu.CompilerParams(
            collective_id=0, has_side_effects=True, vmem_limit_bytes=60 * 1024 * 1024
        ),
    )(query, key, value, output, output_gradient, lse, doc_lengths, w_query, key_weight, value_weight)


def solution(mesh):
    both = P("seq", "head")
    in_specs = (both,) * 5 + (P("head", "seq"), P()) + (both,) * 3
    return jax.shard_map(shards, mesh=mesh, in_specs=in_specs, out_specs=both, check_vma=False)
```

time: 106 us -> 99.1 us (0.935)
  Pallas kernels: 103 us -> 96.7 us
    pallas_call x1, Pallas kernels: 103 us -> 96.7 us  [shards(): pl.pallas_call(functools.partial(kernel, plan), out_shape=jax.ShapeDtypeS...]
where the time goes in v3:
time: 99.1 us; the launch traced here: 98.8 us
  Pallas kernels  96.7 us (98%)
  local copies, waits for them, and re-layouts  2.16 us (2%)
    pallas_call x1, Pallas kernels, shards(): pl.pallas_call(functools.partial(kernel, plan), out_shape=jax.ShapeDtypeS...  96.7 us
    unnamed x1, local copies, waits for them, and re-layouts  2.16 us

profile of v3, /device:TPU:1, one launch (start us, length us, event | category | flops | bytes accessed | tf_op | source)
XLA Modules:
  0.0 98.8 jit_solution(3474998053581292636)
XLA Ops:
  0.0 96.7 %shard_map.100 = bf16[256,1792]{1,0:T(8,128)(2,1)} custom-call(bf16[256,1792]{1,0:T(8,128)(2,1)} %q_hbm.1, bf16[256,256]{1,0:T(8,128)(2,1)} %k_hbm.1, bf16[256,256]{1,0:T(8,128)(2,1)} %v_hbm.1, bf16[256,1792]{1,0:T(8,128)(2,1)} %o_hbm.1, bf16[256,1792]{1,0:T(8,128)(2,1)} %do_hbm.1, f32[14,256]{1,0:T(8,128)} %lse_hbm.1, s32[32]{0:T(128)} %dl_ref.1, ...), custom_call_target="tpu_custom_call" | custom-call | tf_op jit(solution)/shard_map/pallas_call | solution.py:454
  96.7 2.2 %copy.12 = bf16[256,1792]{1,0:T(8,128)(2,1)} copy(bf16[256,1792]{1,0:T(8,128)(2,1)} %shard_map.100) | data formatting | bytes 1835008

commit v4 on v3

--- a/solution.py
+++ b/solution.py
@@ -16,9 +16,10 @@
 BF16 = jnp.bfloat16
 
 NY, NZ = 4, 8
-LINK = 90e3
-HOP = 2.0
-LOOK = 4.0
+LINK = 92e3
+HOP = 2.2
+LOOK = 10.0
+SIB_AFTER = 0.3
 NT = (((1,), (1,)), ((), ()))
 
 
@@ -53,41 +54,45 @@
     return near_z, near_y, part
 
 
-def event_plan(size0, size1):
+def event_plan(size0, size1, extra):
     size = (size0, size1)
-    free = {"z": 0.0, "y": 0.0}
-    queue = {"z": [], "y": []}
-    ops = []
-
-    def arrive(t, part, my, mz):
-        ops.append((t, 0, "recv", part, my, mz))
-        for axis, way, ry, rz in chunk_sends(part, my, mz):
-            first = (part == 1) == (axis == "z")
-            queue[axis].append((t, (0 if first else 1,) + priority(part, ry, rz), (part, my, mz, axis, way, ry, rz)))
-
-    pending = []
-    arrive(0.0, 1, 0, 0)
-    arrive(0.0, 0, 0, 0)
-    while pending or queue["z"] or queue["y"]:
+    links = [(axis, way) for axis in ("z", "y") for way in (1, -1)]
+    free = dict.fromkeys(links, 0.0)
+    free["z", 1] = 2.5
+    queue = {link: [] for link in links}
+    queue["z", -1] += [(extra[0], (-1,), None, c, extra[1]) for c in range(2)]
+    recv, ready_at, begin = {}, {}, {}
+    pending = [(own_at, c, part, 0, 0) for c in range(2) for part, own_at in ((0, 0.0), (1, 2.0))]
+    while pending or any(queue.values()):
         best = None
-        for axis in ("z", "y"):
-            if queue[axis]:
-                start = max(free[axis], min(r for r, _, _ in queue[axis]))
+        for link in links:
+            if queue[link]:
+                start = max(free[link], min(q[0] for q in queue[link]))
                 if best is None or start < best[0]:
-                    best = (start, axis)
+                    best = (start, link)
         if pending and (best is None or min(pending)[0] <= best[0]):
             item = min(pending)
             pending.remove(item)
-            arrive(*item)
+            t, c, part, my, mz = item
+            recv[part, my, mz] = max(t, recv.get((part, my, mz), 0.0))
+            for axis, way, ry, rz in chunk_sends(part, my, mz):
+                first = (part == 1) == (axis == "z")
+                send = (part, my, mz, axis, way, ry, rz)
+                link = (axis, way * (1 - 2 * c))
+                queue[link].append((t, (0 if first else 1,) + priority(part, ry, rz), send, c, size[part]))
             continue
-        start, axis = best
-        item = min((q for q in queue[axis] if q[0] <= start), key=lambda q: q[1])
-        queue[axis].remove(item)
-        ready, _, send = item
-        done = start + size[send[0]] / LINK
-        free[axis] = done
-        pending.append((done + HOP, send[0], send[5], send[6]))
-        ops.append((max(ready, start - LOOK), 1, "send") + send)
+        start, link = best
+        item = min((q for q in queue[link] if q[0] <= start), key=lambda q: q[1])
+        queue[link].remove(item)
+        _, _, send, c, nbytes = item
+        free[link] = start + nbytes / LINK
+        if send is not None:
+            begin.setdefault(send, []).append(start)
+            pending.append((free[link] + HOP, c, send[0], send[5], send[6]))
+    ops = [(t, 0, "recv") + key for key, t in recv.items()]
+    for send, starts in begin.items():
+        ops.append((max(recv[send[:3]], min(starts) - LOOK), 1, "send") + send)
+    ops += [(t + SIB_AFTER, 2, "sib") + key for key, t in recv.items()]
     ops.sort()
     return ops
 
@@ -99,7 +104,7 @@
     qv, ov, dov, kb, vb, kt, bias, stat, lse_v, dq, gt, dk, dv, nsend, nrecv, gsend, grecv,
     own, st, stf, wa, wb, res, psend, precv, oacc,
     in_sem, kv_send, kv_recv, near_send, near_recv, st_send, st_recv, ici_recv, sib_recv,
-    ici_send, sib_send, n_send, n_recv, g_send, g_recv, p_send, p_recv,
+    greet, ici_send, sib_send, n_send, n_recv, g_send, g_recv, p_send, p_recv,
 ):
     tok = qv.shape[0]
     heads = qv.shape[1] // HEAD
@@ -141,7 +146,10 @@
     nxt, prv = lax.rem(me + 2, n), lax.rem(me + n - 2, n)
 
     barrier = pltpu.get_barrier_semaphore()
-    partners = [sib, xsame, xother, zn(1), zn(-1), yn(1), yn(-1), nxt, prv]
+    def xy(d):
+        return at(1 - xc, lax.rem(yc + d + NY, NY), zc, core)
+
+    partners = [sib, xsame, xother, zn(1), zn(-1), yn(1), yn(-1), xy(1), xy(-1)]
     for d in partners:
         pl.semaphore_signal(barrier, inc=1, device_id={"seq": d}, device_id_type=pl.DeviceIdType.MESH)
     pl.semaphore_signal(barrier, inc=1, device_id={"head": 1 - hd}, device_id_type=pl.DeviceIdType.MESH)
@@ -190,17 +198,25 @@
             device_id=dev, device_id_type=pl.DeviceIdType.MESH,
         )
 
-    stage = [
-        remote(own.at[kh], st.at[piece_me], st_send.at[j], st_recv.at[j], {"seq": dev})
-        for j, (kh, dev) in enumerate(((core, xsame), (1 - core, xother), (1 - core, sib)))
-    ]
+    la, lb = wa.shape[3], wb.shape[3]
+    for d in (1, -1):
+        pl.semaphore_signal(greet, inc=1, device_id={"seq": zn(d)}, device_id_type=pl.DeviceIdType.MESH)
+    stage = []
+    for part, cols in enumerate((pl.ds(0, la), pl.ds(la, lb))):
+        for j, (kh, dev) in enumerate(((core, xsame), (1 - core, xother), (1 - core, sib))):
+            stage.append(
+                remote(own.at[kh, :, cols], st.at[piece_me, :, cols], st_send.at[part, j], st_recv.at[part, j], {"seq": dev})
+            )
     halo = [
         remote(src.at[0], src.at[2], kv_send.at[j], kv_recv.at[j], {"seq": nxt}) for j, src in enumerate((kb, vb))
     ]
-    for c in stage + halo:
+    for c in stage:
         c.start()
     mine_in = pltpu.make_async_copy(own.at[core], st.at[piece_me], in_sem.at[10])
     mine_in.start()
+    pl.semaphore_wait(greet, 2)
+    for c in halo:
+        c.start()
 
     def near_copy(j, src, b):
         return remote(src.at[b], src.at[1], near_send.at[j], near_recv.at[j], {"seq": sib})
@@ -209,15 +225,6 @@
     def _():
         for j, src in enumerate((kb, vb)):
             near_copy(j, src, 0).start()
-
-    for c in stage:
-        c.wait_recv()
-    mine_in.wait()
-    la, lb = wa.shape[3], wb.shape[3]
-    for p in range(4):
-        stf[pl.ds(p * rows, rows), :] = st[p].astype(F32)
-    wb[core, slot_me] = stf[:, pl.ds(la, lb)].astype(BF16)
-    wa[core, slot_me] = stf[:, pl.ds(0, la)].astype(BF16)
 
     def event(kind, part, my, mz, *to):
         buf = wb if part == 1 else wa
@@ -225,15 +232,24 @@
         if kind == "recv":
             if (my, mz) != (0, 0):
                 remote(ref, ref, ici_send.at[part], ici_recv.at[part, my, mz], {"seq": sib}).wait_recv()
+        elif kind == "sib":
             remote(ref, ref, sib_send.at[part], sib_recv.at[part, my, mz], {"seq": sib}).start()
         else:
             axis, way, ry, rz = to
             dev = zn(way) if axis == "z" else yn(way)
             remote(ref, ref, ici_send.at[part], ici_recv.at[part, ry, rz], {"seq": dev}).start()
 
-    attn_at, by_group = plan
-    for ev in attn_at[-1]:
-        event(*ev)
+    attn_at, mid, by_group = plan
+    mine_in.wait()
+    for part, (buf, cols) in enumerate(((wa, pl.ds(0, la)), (wb, pl.ds(la, lb)))):
+        for c in stage[3 * part : 3 * part + 3]:
+            c.wait_recv()
+        for p in range(4):
+            stf[pl.ds(p * rows, rows), cols] = st[p, :, cols].astype(F32)
+        buf[core, slot_me] = stf[:, cols].astype(BF16)
+        for ev in attn_at[-1]:
+            if ev[1] == part:
+                event(*ev)
 
     for c in locals_:
         c.wait()
@@ -336,6 +352,8 @@
 
     lax.fori_loop(0, heads, to_gt, 0)
 
+    for ev in mid:
+        event(*ev)
     far_grad.wait_recv()
     for j, acc in enumerate((dk, dv)):
         for g in range(groups):
@@ -409,33 +427,34 @@
         remote(psend.at[j], precv.at[j], p_send.at[j], p_recv.at[j], {"head": 1 - hd}).wait_send()
 
 
-def make_plan(size0, size1, steps, attn_start, attn_us):
-    order = [op[2:] for op in event_plan(size0, size1)]
-    times = [op[0] for op in event_plan(size0, size1)]
-    attn_at = {}
-    left = []
-    for t, op in zip(times, order):
+def make_plan(size0, size1, halo, steps, attn_start, attn_us, gt_at):
+    ops = event_plan(size0, size1, (attn_start + attn_us * (steps - 4), halo))
+    attn_at = {-1: []}
+    mid, left = [], []
+    for t, _, *op in ops:
         s = math.ceil((t - attn_start) / attn_us)
-        if t <= 0.0:
-            attn_at.setdefault(-1, []).append(op)
+        if s < 0:
+            attn_at[-1].append(op)
         elif s < steps:
-            attn_at.setdefault(max(s, 0), []).append(op)
+            attn_at.setdefault(s, []).append(op)
+        elif t < gt_at:
+            mid.append(op)
         else:
-            left.append((t, op))
-    early, late = [], [[] for _ in range(NZ)]
+            left.append(op)
+    late = [[] for _ in range(NZ)]
     rank = {0: 0, 1: 1, 7: 2, 2: 3, 6: 4, 3: 5, 5: 6, 4: 7}
     pos = 0
     for j in range(NZ):
         need = -1
-        for i, (_, op) in enumerate(left):
-            if op[0] == "recv" and (rank[op[3]] <= j or rank[(NZ - op[3]) % NZ] <= j):
+        for i, op in enumerate(left):
+            if op[0] == "sib" and (rank[op[3]] <= j or rank[(NZ - op[3]) % NZ] <= j):
                 need = i
         if j == NZ - 1:
             need = len(left) - 1
         while pos <= need:
-            late[j].append(left[pos][1])
+            late[j].append(left[pos])
             pos += 1
-    return attn_at, late
+    return attn_at, mid, late
 
 
 def shards(query, key, value, output, output_gradient, lse, doc_lengths, w_query, key_weight, value_weight):
@@ -447,13 +466,14 @@
     la = kdim // 6
     lb = kdim // 3
     slots = NY * NZ
-    plan = make_plan(4 * rows * la * 2, 4 * rows * lb * 2, 9 * groups, 4.0, 0.9)
+    halo = 2 * tok * groups * HEAD * 2
+    plan = make_plan(4 * rows * la * 2, 4 * rows * lb * 2, halo, 9 * groups, 3.0, 0.6, 20.0)
     any_ = pl.BlockSpec(memory_space=pl.ANY)
     vmem = pl.BlockSpec(memory_space=pltpu.VMEM)
     dma = pltpu.SemaphoreType.DMA
     return pl.pallas_call(
         functools.partial(kernel, plan),
-        out_shape=jax.ShapeDtypeStruct((tok, query.shape[1]), BF16),
+        out_shape=pltpu.VMEM((tok, query.shape[1]), BF16),
         in_specs=[any_] * 6 + [pl.BlockSpec(memory_space=pltpu.SMEM)] + [any_] * 3,
         out_specs=vmem,
         scratch_shapes=[
@@ -483,8 +503,8 @@
             pltpu.VMEM((NZ, NY * 2 * rows, tok), BF16),
             pltpu.VMEM((NZ, NY * 2 * rows, tok), BF16),
             pltpu.VMEM((slots * 2 * rows, tok), F32),
-            dma((11,)), dma((2,)), dma((2,)), dma((2,)), dma((2,)), dma((3,)), dma((3,)),
-            dma((2, NY, NZ)), dma((2, NY, NZ)),
+            dma((11,)), dma((2,)), dma((2,)), dma((2,)), dma((2,)), dma((2, 3)), dma((2, 3)),
+            dma((2, NY, NZ)), dma((2, NY, NZ)), pltpu.SemaphoreType.REGULAR,
             dma((2,)), dma((2,)), dma(()), dma(()), dma(()), dma(()), dma((NZ,)), dma((NZ,)),
         ],
         compiler_params=pltpu.CompilerParams(

time: 99.1 us -> 93.1 us (0.939)
  Pallas kernels: 96.7 us -> 92 us
  local copies, waits for them, and re-layouts: 2.16 us -> 0.93 us
    pallas_call x1, Pallas kernels: 96.7 us -> 92 us  [shards(): pl.pallas_call(functools.partial(kernel, plan), out_shape=pltpu.VMEM((tok...]
    unnamed x1, local copies, waits for them, and re-layouts: 2.16 us -> 0.93 us
where the time goes in v4:
time: 93.1 us; the launch traced here: 93 us
  Pallas kernels  92 us (99%)
    pallas_call x1, Pallas kernels, shards(): pl.pallas_call(functools.partial(kernel, plan), out_shape=pltpu.VMEM((tok...  92 us

profile of v4, /device:TPU:1, one launch (start us, length us, event | category | flops | bytes accessed | tf_op | source)
XLA Modules:
  0.0 93.0 jit_solution(6788842129722902555)
XLA Ops:
  0.0 92.0 %shard_map.100 = bf16[256,1792]{1,0:T(8,128)(2,1)S(1)} custom-call(bf16[256,1792]{1,0:T(8,128)(2,1)} %q_hbm.1, bf16[256,256]{1,0:T(8,128)(2,1)} %k_hbm.1, bf16[256,256]{1,0:T(8,128)(2,1)} %v_hbm.1, bf16[256,1792]{1,0:T(8,128)(2,1)} %o_hbm.1, bf16[256,1792]{1,0:T(8,128)(2,1)} %do_hbm.1, f32[14,256]{1,0:T(8,128)} %lse_hbm.1, s32[32]{0:T(128)} %dl_ref.1, ...), custom_call_target="tpu_custom_call" | custom-call | tf_op jit(solution)/shard_map/pallas_call | solution.py:474
  92.1 0.9 copy.12

commit v5 on v4

--- a/solution.py
+++ b/solution.py
@@ -19,7 +19,7 @@
 LINK = 92e3
 HOP = 2.2
 LOOK = 10.0
-SIB_AFTER = 0.3
+RANK = {0: 0, 1: 1, 7: 2, 2: 3, 6: 4, 3: 5, 5: 6, 4: 7}
 NT = (((1,), (1,)), ((), ()))
 
 
@@ -30,7 +30,7 @@
     y_up = ("y", 1, (my + 1) % NY, mz)
     y_dn = ("y", -1, (my - 1) % NY, mz)
     z_ups = mz <= 3
-    z_dns = mz == 0 or mz in (6, 7)
+    z_dns = mz == 0 or mz in (5, 6, 7)
     y_ups = my <= 1
     y_dns = my == 0
     if part == 1:
@@ -49,9 +49,11 @@
 
 
 def priority(part, my, mz):
-    near_z = min(mz, NZ - mz)
-    near_y = min(my, NY - my)
-    return near_z, near_y, part
+    return RANK[mz], min(my, NY - my), part
+
+
+def takes(core, axis, way, rz):
+    return axis != "z" or rz != NZ // 2 or (way == 1) == (core == 0)
 
 
 def event_plan(size0, size1, extra):
@@ -76,9 +78,11 @@
             t, c, part, my, mz = item
             recv[part, my, mz] = max(t, recv.get((part, my, mz), 0.0))
             for axis, way, ry, rz in chunk_sends(part, my, mz):
+                if not takes(c, axis, way, rz):
+                    continue
                 first = (part == 1) == (axis == "z")
                 send = (part, my, mz, axis, way, ry, rz)
-                link = (axis, way * (1 - 2 * c))
+                link = (axis, way * (1 - 2 * c) if axis == "y" else way)
                 queue[link].append((t, (0 if first else 1,) + priority(part, ry, rz), send, c, size[part]))
             continue
         start, link = best
@@ -92,7 +96,6 @@
     ops = [(t, 0, "recv") + key for key, t in recv.items()]
     for send, starts in begin.items():
         ops.append((max(recv[send[:3]], min(starts) - LOOK), 1, "send") + send)
-    ops += [(t + SIB_AFTER, 2, "sib") + key for key, t in recv.items()]
     ops.sort()
     return ops
 
@@ -102,15 +105,16 @@
     q_hbm, k_hbm, v_hbm, o_hbm, do_hbm, lse_hbm, dl_ref, wq_hbm, wk_hbm, wv_hbm,
     out_ref,
     qv, ov, dov, kb, vb, kt, bias, stat, lse_v, dq, gt, dk, dv, nsend, nrecv, gsend, grecv,
-    own, st, stf, wa, wb, res, psend, precv, oacc,
-    in_sem, kv_send, kv_recv, near_send, near_recv, st_send, st_recv, ici_recv, sib_recv,
-    greet, ici_send, sib_send, n_send, n_recv, g_send, g_recv, p_send, p_recv,
+    own, st, stf, wa, wb, gx, psum, ssend, srecv, psend, precv, oacc,
+    in_sem, kv_send, kv_recv, near_send, near_recv, st_send, st_recv, ici_recv,
+    greet, ici_send, gx_send, gx_recv, s_send, s_recv, n_send, n_recv, g_send, g_recv, p_send, p_recv,
 ):
     tok = qv.shape[0]
     heads = qv.shape[1] // HEAD
     groups = kb.shape[2] // HEAD
     per = heads // groups
     rows, hw = st.shape[1], st.shape[2]
+    kh_heads = hw // HEAD
     half = 2 * rows
     scale = 1.0 / math.sqrt(HEAD)
     wq_w, wk_w = wq_hbm.shape[1], wk_hbm.shape[1]
@@ -123,22 +127,21 @@
     yc = lax.rem(me // (2 * NZ), NY)
     xc = me // (2 * NZ * NY)
     sg = 1 - 2 * core
-    slot_me = yc * NZ + zc
     piece_me = xc * 2 + core
 
     def at(x, y, z, c):
         return ((x * NY + y) * NZ + z) * 2 + c
 
     def zn(d):
-        return at(xc, yc, lax.rem(zc + d * sg + NZ, NZ), core)
+        return at(xc, yc, lax.rem(zc + d + NZ, NZ), core)
 
     def yn(d):
         return at(xc, lax.rem(yc + d * sg + NY, NY), zc, core)
 
     def slot_of(my, mz):
         y = lax.rem(yc - my * sg + NY, NY)
-        z = lax.rem(zc - mz * sg + NZ, NZ)
-        return y * NZ + z
+        z = lax.rem(zc - mz + NZ, NZ)
+        return z * NY + y
 
     sib = at(xc, yc, zc, 1 - core)
     xsame = at(1 - xc, yc, zc, core)
@@ -198,7 +201,7 @@
             device_id=dev, device_id_type=pl.DeviceIdType.MESH,
         )
 
-    la, lb = wa.shape[3], wb.shape[3]
+    la, lb = wa.shape[2], wb.shape[2]
     for d in (1, -1):
         pl.semaphore_signal(greet, inc=1, device_id={"seq": zn(d)}, device_id_type=pl.DeviceIdType.MESH)
     stage = []
@@ -228,25 +231,27 @@
 
     def event(kind, part, my, mz, *to):
         buf = wb if part == 1 else wa
-        ref = buf.at[core, slot_of(my, mz)]
+        ref = buf.at[slot_of(my, mz)]
         if kind == "recv":
             if (my, mz) != (0, 0):
                 remote(ref, ref, ici_send.at[part], ici_recv.at[part, my, mz], {"seq": sib}).wait_recv()
-        elif kind == "sib":
-            remote(ref, ref, sib_send.at[part], sib_recv.at[part, my, mz], {"seq": sib}).start()
         else:
             axis, way, ry, rz = to
             dev = zn(way) if axis == "z" else yn(way)
-            remote(ref, ref, ici_send.at[part], ici_recv.at[part, ry, rz], {"seq": dev}).start()
-
-    attn_at, mid, by_group = plan
+            copy = remote(ref, ref, ici_send.at[part], ici_recv.at[part, ry, rz], {"seq": dev})
+            if axis == "z" and rz == NZ // 2:
+                pl.when(core == (0 if way == 1 else 1))(copy.start)
+            else:
+                copy.start()
+
+    attn_at, mid, by_group, rest = plan
     mine_in.wait()
     for part, (buf, cols) in enumerate(((wa, pl.ds(0, la)), (wb, pl.ds(la, lb)))):
         for c in stage[3 * part : 3 * part + 3]:
             c.wait_recv()
         for p in range(4):
             stf[pl.ds(p * rows, rows), cols] = st[p, :, cols].astype(F32)
-        buf[core, slot_me] = stf[:, cols].astype(BF16)
+        buf[zc * NY + yc] = stf[:, cols].astype(BF16)
         for ev in attn_at[-1]:
             if ev[1] == part:
                 event(*ev)
@@ -347,7 +352,7 @@
     lax.fori_loop(0, outer, attn_step, 0)
 
     def to_gt(h, _):
-        gt[pl.ds(pl.multiple_of(h * HEAD, HEAD), HEAD), :] = dq[h].astype(BF16)
+        gt[h // kh_heads, pl.ds(pl.multiple_of(lax.rem(h, kh_heads) * HEAD, HEAD), HEAD), :] = dq[h].astype(BF16)
         return 0
 
     lax.fori_loop(0, heads, to_gt, 0)
@@ -359,72 +364,132 @@
         for g in range(groups):
             c0 = cols_of(j, g)
             tot = acc[0, g] + grecv[:, c0].astype(F32) + jnp.where(core == 0, nrecv[:, c0], 0.0)
-            gt[pl.ds((heads + j * groups + g) * HEAD, HEAD), :] = tot.T.astype(BF16)
+            gt[1, pl.ds((heads + j * groups + g - kh_heads) * HEAD, HEAD), :] = tot.T.astype(BF16)
+    gx_copy = remote(gt.at[1 - core], gx, gx_send, gx_recv, {"seq": sib})
+    gx_copy.start()
+    gx_copy.wait_recv()
 
     def group_mz(j):
         return lax.rem(jnp.where(lax.rem(j, 2) == 1, (j + 1) // 2, NZ - j // 2), NZ)
 
-    def sib_wait(part, my, mz):
-        buf = wb if part == 1 else wa
-        ref = buf.at[core, slot_me]
-        remote(ref, ref, sib_send.at[part], sib_recv.at[part, my, mz], {"seq": sib}).wait_recv()
+    def z_of(j):
+        return lax.rem(zc - group_mz(j) + NZ, NZ)
+
+    def quad(za):
+        return pl.ds(za * NY, NY)
+
+    def sums(where, k):
+        return remote(ssend.at[where], srecv.at[where], s_send.at[k], s_recv.at[k], {"seq": sib})
+
+    def across(where, k):
+        return remote(psend.at[where], precv.at[where], p_send.at[k], p_recv.at[k], {"head": 1 - hd})
+
+    def orow(y, za):
+        return pl.ds(pl.multiple_of((y * NZ + za) * half, 8), half)
+
+    def total(y, za):
+        slot = za * NY + y
+        tot = psum[slot] + srecv[slot].astype(F32)
+        lo, hi = tot[:half], tot[half:]
+        oacc[orow(y, za), :] = jnp.where(hd == 0, lo, hi)
+        psend[slot] = jnp.where(hd == 0, hi, lo).astype(BF16)
+
+    def add(y, za):
+        oacc[orow(y, za), :] = oacc[orow(y, za), :] + precv[za * NY + y].astype(F32)
+
+    def multiply(ys, za):
+        slots = [za * NY + y for y in ys]
+        lhs = jnp.concatenate([jnp.concatenate([wa[i], wb[i]], axis=1) for i in slots], axis=0)
+        n_rows = 4 * rows
+        other = jnp.dot(lhs, gx[...], preferred_element_type=F32).astype(BF16)
+        for k, i in enumerate(slots):
+            ssend[i] = other[k * n_rows : (k + 1) * n_rows]
+        return lhs, slots, n_rows
+
+    def keep(lhs, slots, n_rows):
+        mine = jnp.dot(lhs, gt[core], preferred_element_type=F32)
+        for k, i in enumerate(slots):
+            psum[i] = mine[k * n_rows : (k + 1) * n_rows]
+
+    def late_op(kind, j):
+        za = z_of(jnp.int32(j))
+        if kind == "sum":
+            sums(quad(za), za).wait_recv()
+            for y in range(NY):
+                total(y, za)
+            across(quad(za), za).start()
+        else:
+            across(quad(za), za).wait_recv()
+            for y in range(NY):
+                add(y, za)
+
+    def run(ops):
+        for ev in ops:
+            if ev[0] in ("sum", "add"):
+                late_op(*ev)
+            else:
+                event(*ev)
 
     def project(j, _):
-        for jj in range(NZ):
-            @pl.when(j == jj)
-            def _(jj=jj):
-                mzs = (jj + 1) // 2 if jj % 2 else (NZ - jj // 2) % NZ
-                for ev in by_group[jj]:
-                    event(*ev)
-                for part in range(2):
-                    for my in range(NY):
-                        sib_wait(part, (NY - my) % NY, (NZ - mzs) % NZ)
-        mz = group_mz(j)
-        parts = []
-        for my in range(NY):
-            s = slot_of(my, mz)
-            parts.append(jnp.concatenate([wa[0, s], wb[0, s], wa[1, s], wb[1, s]], axis=1))
-        lhs = jnp.concatenate(parts, axis=0)
-        res[...] = jnp.dot(lhs, gt[...], preferred_element_type=F32)
-        out = []
-        for my in range(NY):
-            s = slot_of(my, mz)
-            mine = pl.multiple_of(my * 2 * half + half * hd, 8)
-            oth = pl.multiple_of(my * 2 * half + half * (1 - hd), 8)
-            oacc[pl.ds(pl.multiple_of(s * half, 8), half), :] = res[pl.ds(mine, half), :]
-            out.append(res[pl.ds(oth, half), :])
-        psend[j] = jnp.concatenate(out, axis=0).astype(BF16)
-        remote(psend.at[j], precv.at[j], p_send.at[j], p_recv.at[j], {"head": 1 - hd}).start()
+        for jj in range(NZ - 1):
+            if by_group[jj]:
+                @pl.when(j == jj)
+                def _(jj=jj):
+                    run(by_group[jj])
+        za = z_of(j)
+        state = multiply(list(range(NY)), za)
+        sums(quad(za), za).start()
+        keep(*state)
         return 0
-
-    lax.fori_loop(0, NZ, project, 0)
-
-    def finish(j, _):
-        remote(psend.at[j], precv.at[j], p_send.at[j], p_recv.at[j], {"head": 1 - hd}).wait_recv()
-        mz = group_mz(j)
-        got = precv[j].astype(F32)
-        for my in range(NY):
-            r = pl.ds(pl.multiple_of(slot_of(my, mz) * half, 8), half)
-            oacc[r, :] = oacc[r, :] + got[my * half : (my + 1) * half]
-        return 0
-
-    lax.fori_loop(0, NZ, finish, 0)
 
     def flip(k, _):
         c = pl.ds(pl.multiple_of(k * HEAD, HEAD), HEAD)
         out_ref[:, c] = oacc[c, :].T.astype(BF16)
         return 0
 
+    lax.fori_loop(0, NZ - 1, project, 0)
+
+    last = lax.rem(zc + NZ // 2, NZ)
+    far_y = lax.rem(yc + NY // 2, NY)
+    near_ys = [lax.rem(yc + d, NY) for d in range(NY) if d != NY // 2]
+    run(by_group[NZ - 1])
+    state = multiply(near_ys, last)
+    for y in near_ys:
+        sums(last * NY + y, NZ + y).start()
+    keep(*state)
+    run(by_group[NZ])
+    state = multiply([far_y], last)
+    sums(last * NY + far_y, NZ + far_y).start()
+    keep(*state)
+    run([op for op in rest if op[0] == "sum"])
+    for y in near_ys + [far_y]:
+        sums(last * NY + y, NZ + y).wait_recv()
+        total(y, last)
+        across(last * NY + y, NZ + y).start()
+    run([op for op in rest if op[0] == "add"])
+    for y in near_ys:
+        across(last * NY + y, NZ + y).wait_recv()
+        add(y, last)
     lax.fori_loop(0, oacc.shape[0] // HEAD, flip, 0)
+    across(last * NY + far_y, NZ + far_y).wait_recv()
+    add(far_y, last)
+    first_row = (far_y * NZ + last) * half
+    flip(first_row // HEAD, 0)
+    flip((first_row + half - 1) // HEAD, 0)
 
     for c in stage + halo + [near_copy(0, kb, 0), near_copy(1, vb, 0), near_grad, far_grad]:
         c.wait_send()
-    for part, buf in ((0, wa), (1, wb)):
-        for sem, count in ((ici_send, NY * NZ - 1), (sib_send, NY * NZ)):
-            many = buf.at[0, pl.ds(0, count)]
-            remote(many, many, sem.at[part], ici_recv.at[part, 0, 0], {"seq": sib}).wait_send()
-    for j in range(NZ):
-        remote(psend.at[j], precv.at[j], p_send.at[j], p_recv.at[j], {"head": 1 - hd}).wait_send()
+    gx_copy.wait_send()
+    for pt, buf in ((0, wa), (1, wb)):
+        many = buf.at[pl.ds(0, NY * NZ - 1)]
+        remote(many, many, ici_send.at[pt], ici_recv.at[pt, 0, 0], {"seq": sib}).wait_send()
+    for j in range(NZ - 1):
+        za = z_of(jnp.int32(j))
+        sums(quad(za), za).wait_send()
+        across(quad(za), za).wait_send()
+    for y in range(NY):
+        sums(last * NY + y, NZ + y).wait_send()
+        across(last * NY + y, NZ + y).wait_send()
 
 
 def make_plan(size0, size1, halo, steps, attn_start, attn_us, gt_at):
@@ -440,21 +505,38 @@
         elif t < gt_at:
             mid.append(op)
         else:
-            left.append(op)
-    late = [[] for _ in range(NZ)]
-    rank = {0: 0, 1: 1, 7: 2, 2: 3, 6: 4, 3: 5, 5: 6, 4: 7}
+            left.append((t, op))
+    stages = NZ + 1
+    need = [-1] * stages
+    at = [0.0] * stages
+    for j in range(stages):
+        for i, (t, op) in enumerate(left):
+            rank = stages - 1 if op[2:4] == [NY // 2, NZ // 2] else RANK[op[3]]
+            if op[0] == "recv" and rank <= j:
+                need[j] = i
+        at[j] = max(left[need[j]][0] if need[j] >= 0 else 0.0, gt_at + 1.5 * (j + 1))
+    late = [[] for _ in range(stages)]
+    extra = []
+    for j in range(NZ - 1):
+        t = at[j] + 3.0
+        extra += [(t, j + 1, ["sum", j]), (t + 6.0, j + 1, ["add", j])]
+    extra.sort()
     pos = 0
-    for j in range(NZ):
-        need = -1
-        for i, op in enumerate(left):
-            if op[0] == "sib" and (rank[op[3]] <= j or rank[(NZ - op[3]) % NZ] <= j):
-                need = i
-        if j == NZ - 1:
-            need = len(left) - 1
-        while pos <= need:
-            late[j].append(left[pos])
-            pos += 1
-    return attn_at, mid, late
+    for j in range(stages):
+        upto = need[j] if j < stages - 1 else len(left) - 1
+        while True:
+            ev = left[pos] if pos <= upto else None
+            ex = extra[0] if extra and extra[0][1] <= j else None
+            if ex and ex[0] < (ev[0] if ev else at[j]):
+                late[j].append(ex[2])
+                extra.pop(0)
+            elif ev:
+                late[j].append(ev[1])
+                pos += 1
+            else:
+                break
+    assert pos == len(left)
+    return attn_at, mid, late, [ex[2] for ex in extra]
 
 
 def shards(query, key, value, output, output_gradient, lse, doc_lengths, w_query, key_weight, value_weight):
@@ -487,7 +569,7 @@
             pltpu.VMEM((heads, 8, tok), F32),
             pltpu.VMEM((heads, tok), F32),
             pltpu.VMEM((heads, HEAD, tok), F32),
-            pltpu.VMEM((kdim, tok), BF16),
+            pltpu.VMEM((2, kdim // 2, tok), BF16),
             pltpu.VMEM((3, groups, tok, HEAD), F32),
             pltpu.VMEM((3, groups, tok, HEAD), F32),
             pltpu.VMEM((tok, 2 * groups * HEAD), F32),
@@ -497,15 +579,18 @@
             pltpu.VMEM((2, rows, kdim // 2), BF16),
             pltpu.VMEM((4, rows, kdim // 2), BF16),
             pltpu.VMEM((4 * rows, kdim // 2), F32),
-            pltpu.VMEM((2, slots, 4 * rows, la), BF16),
-            pltpu.VMEM((2, slots, 4 * rows, lb), BF16),
-            pltpu.VMEM((NY * 4 * rows, tok), F32),
-            pltpu.VMEM((NZ, NY * 2 * rows, tok), BF16),
-            pltpu.VMEM((NZ, NY * 2 * rows, tok), BF16),
+            pltpu.VMEM((slots, 4 * rows, la), BF16),
+            pltpu.VMEM((slots, 4 * rows, lb), BF16),
+            pltpu.VMEM((kdim // 2, tok), BF16),
+            pltpu.VMEM((slots, 4 * rows, tok), F32),
+            pltpu.VMEM((slots, 4 * rows, tok), BF16),
+            pltpu.VMEM((slots, 4 * rows, tok), BF16),
+            pltpu.VMEM((slots, 2 * rows, tok), BF16),
+            pltpu.VMEM((slots, 2 * rows, tok), BF16),
             pltpu.VMEM((slots * 2 * rows, tok), F32),
             dma((11,)), dma((2,)), dma((2,)), dma((2,)), dma((2,)), dma((2, 3)), dma((2, 3)),
-            dma((2, NY, NZ)), dma((2, NY, NZ)), pltpu.SemaphoreType.REGULAR,
-            dma((2,)), dma((2,)), dma(()), dma(()), dma(()), dma(()), dma((NZ,)), dma((NZ,)),
+            dma((2, NY, NZ)), pltpu.SemaphoreType.REGULAR,
+            dma((2,)), dma(()), dma(()), dma((NZ + NY,)), dma((NZ + NY,)), dma(()), dma(()), dma(()), dma(()), dma((NZ + NY,)), dma((NZ + NY,)),
         ],
         compiler_params=pltpu.CompilerParams(
             collective_id=0, has_side_effects=True, vmem_limit_bytes=60 * 1024 * 1024

time: 93.1 us -> 88.5 us (0.951)
  Pallas kernels: 92 us -> 87.5 us
    pallas_call x1, Pallas kernels: 92 us -> 87.5 us  [shards(): pl.pallas_call(functools.partial(kernel, plan), out_shape=pltpu.VMEM((tok...]
where the time goes in v5:
time: 88.5 us
  Pallas kernels  87.5 us (99%)
  local copies, waits for them, and re-layouts  0.93 us (1%)
    pallas_call x1, Pallas kernels, shards(): pl.pallas_call(functools.partial(kernel, plan), out_shape=pltpu.VMEM((tok...  87.5 us

profile of v5, /device:TPU:1, one launch (start us, length us, event | category | flops | bytes accessed | tf_op | source)
XLA Modules:
  0.0 88.5 jit_solution(9657262697440788547)
XLA Ops:
  0.0 87.5 %shard_map.100 = bf16[256,1792]{1,0:T(8,128)(2,1)S(1)} custom-call(bf16[256,1792]{1,0:T(8,128)(2,1)} %q_hbm.1, bf16[256,256]{1,0:T(8,128)(2,1)} %k_hbm.1, bf16[256,256]{1,0:T(8,128)(2,1)} %v_hbm.1, bf16[256,1792]{1,0:T(8,128)(2,1)} %o_hbm.1, bf16[256,1792]{1,0:T(8,128)(2,1)} %do_hbm.1, f32[14,256]{1,0:T(8,128)} %lse_hbm.1, s32[32]{0:T(128)} %dl_ref.1, ...), custom_call_target="tpu_custom_call" | custom-call | tf_op jit(solution)/shard_map/pallas_call | solution.py:556
  87.5 0.9 %copy.12 = bf16[256,1792]{1,0:T(8,128)(2,1)} copy(bf16[256,1792]{1,0:T(8,128)(2,1)S(1)} %shard_map.100) | data formatting | bytes 1835008
